TPU v7x, 256 devices: a whole 4x4x8 slice. The times are simulated.
256 devices in a mesh: gx: 8 (over y, core), gy: 32 (over x, z).
Axes of the slice: x: 4, y: 4, z: 8, core: 2. Of those that a mesh axis runs over, the one named last changes fastest.
Arguments:
- control: float32 [1, 2, 6, 1536, 3072], P(None, None, None, 'gy', 'gx'), may hold values from -6 to 6
- sigma: float32 [2, 6, 1536, 3072], P(None, None, 'gy', 'gx'), may hold values from 0.5 to 5
- kappa: float32 [5, 1536, 3072], P(None, 'gy', 'gx'), may hold values from 0.05 to 5
- beta: float32 [6, 1536, 3072], P(None, 'gy', 'gx'), may hold values from -3 to 3
- sea_mask: int32 [1536, 3072], P('gy', 'gx'), may hold values 0 or 1
- x_inverse: float32 [3072, 3072], P('gx'), as said below
- y_inverse: float32 [1536, 1536], P('gx')
- ssh_coef: float32 [2, 6], replicated, may hold values from -1.5 to 1.5
- obs_owner: int32 [65536, 1], P(('gx', 'gy')), may hold values from 0 to 255; in each aligned block of 256 rows (0 to 255, 256 to 511, ...) at most 2 rows name the same one
- tile_index: int32 [65536], P(('gx', 'gy')), may hold values from 0 to 18046, as said below
- obs_frac: float32 [2, 65536], P(None, ('gx', 'gy')), may hold values from 0 to 1
- obs_count: int32 [256], P(('gx', 'gy')), may hold values from 128 to 256
Outputs:
- increments: float32 [1, 2, 6, 1536, 3072], P(None, None, None, 'gy', 'gx')
- sea_height: float32 [1, 1536, 3072], P(None, 'gy', 'gx')
- obs_equiv: float32 [2, 13, 65536], P(None, None, ('gx', 'gy'))
Inputs may be any that keep to these rules, and one draw needn't show every extreme that they name: `obs_owner`: among the slots of one device, at most 2 name the same owner. `tile_index`: row * 384 + column of a cell in the device's own tile, with row below 47 and column below 383. `x_inverse`: the zonal inverse is symmetric.
All inputs are finite; a program needn't handle non-finite values. No bound on the sum of `sea_mask` on one device may be relied on, other than what follows from the above.
Results may differ from a plain program's by a relative error of at most 0.00013.
Values sent between devices are 32-bit elements; how exact they have to be, the bound alone decides.
A program may use at most 128 MiB of HBM per device.

v0:
```python
import jax
import jax.numpy as jnp
from jax import lax
from jax.sharding import PartitionSpec as P

STEPS = 2
CAP = 2


def vertical(values, kappa):
    levels = values.shape[2]
    c_list = []
    d_list = []
    for level in range(levels):
        k_below = kappa[level - 1] if level > 0 else 0.0
        k_above = kappa[level] if level < levels - 1 else 0.0
        diag_term = 1.0 + k_below + k_above
        if level == 0:
            pivot = diag_term
            d_new = values[:, :, 0] / pivot
        else:
            pivot = diag_term + k_below * c_list[-1]
            d_new = (values[:, :, level] + k_below * d_list[-1]) / pivot
        c_list.append(-k_above / pivot)
        d_list.append(d_new)
    result = [d_list[-1]]
    for level in range(levels - 2, -1, -1):
        result.insert(0, d_list[level] - c_list[level] * result[0])
    return jnp.stack(result, axis=2)


def body(
    control,
    sigma,
    kappa,
    beta,
    sea_mask,
    x_inverse,
    y_inverse,
    ssh_coef,
    obs_owner,
    tile_index,
    obs_frac,
    obs_count,
):
    highest = lax.Precision.HIGHEST
    vec_count, kinds, levels, lat_rows, lon_cols = control.shape
    field_count = vec_count * kinds * levels
    sea_open = sea_mask.astype(jnp.float32)
    grid_field = control.reshape(field_count, lat_rows, lon_cols)
    whole_y = lax.all_gather(y_inverse, "gx", axis=0, tiled=True)
    for diffusion_step in range(STEPS):
        grid_field = sea_open * jnp.einsum(
            "fyb,ab->fya",
            lax.all_gather(grid_field, "gx", axis=2, tiled=True),
            x_inverse,
            precision=highest,
        )
        turned = jnp.swapaxes(grid_field, 1, 2)
        merid_lines = lax.all_to_all(turned, "gy", split_axis=1, concat_axis=2, tiled=True)
        solved = jnp.einsum("fxb,ab->fxa", merid_lines, whole_y, precision=highest)
        returned = lax.all_to_all(solved, "gy", split_axis=2, concat_axis=1, tiled=True)
        grid_field = sea_open * jnp.swapaxes(returned, 1, 2)
        grid_field = vertical(
            grid_field.reshape(vec_count, kinds, levels, lat_rows, lon_cols), kappa
        ).reshape(field_count, lat_rows, lon_cols)
    grid_field = grid_field.reshape(vec_count, kinds, levels, lat_rows, lon_cols)
    temper = sigma[0] * grid_field[:, 0]
    saline = sigma[1] * grid_field[:, 1] + beta * temper
    height = jnp.sum(
        ssh_coef[0][None, :, None, None] * temper + ssh_coef[1][None, :, None, None] * saline,
        axis=1,
    )
    increments = jnp.stack([temper, saline], axis=1)
    profile = jnp.concatenate([temper, saline, height[:, None]], axis=1)
    slot_total = tile_index.shape[0]
    row_index = tile_index // lon_cols
    col_index = tile_index % lon_cols
    frac_x = obs_frac[0]
    frac_y = obs_frac[1]
    corner_a = profile[:, :, row_index, col_index]
    corner_b = profile[:, :, row_index, col_index + 1]
    corner_c = profile[:, :, row_index + 1, col_index]
    corner_d = profile[:, :, row_index + 1, col_index + 1]
    interp = (1.0 - frac_y) * ((1.0 - frac_x) * corner_a + frac_x * corner_b) + frac_y * (
        (1.0 - frac_x) * corner_c + frac_x * corner_d
    )
    live_slot = (jnp.arange(slot_total, dtype=jnp.int32) < obs_count[0]).astype(jnp.float32)
    record_len = interp.shape[0] * interp.shape[1]
    interp = (interp * live_slot).reshape(record_len, slot_total)
    gx_count = lax.axis_size("gx")
    gy_count = lax.axis_size("gy")
    device_total = gx_count * gy_count
    owners = obs_owner[:, 0]
    one_hot = (owners[:, None] == jnp.arange(device_total, dtype=jnp.int32)[None, :]).astype(
        jnp.int32
    )
    before = jnp.cumsum(one_hot, axis=0) - one_hot
    slot_rank = jnp.sum(before * one_hot, axis=1)
    outgoing = (
        jnp.zeros((CAP, record_len, device_total), jnp.float32)
        .at[slot_rank, :, owners]
        .set(interp.T)
    )
    outgoing = outgoing.reshape(CAP, record_len, gx_count, gy_count)
    arrived = lax.all_to_all(
        lax.all_to_all(outgoing, "gx", split_axis=2, concat_axis=2, tiled=True),
        "gy",
        split_axis=3,
        concat_axis=3,
        tiled=True,
    )
    obs_equiv = arrived.reshape(CAP, record_len, device_total)
    return (increments, height, obs_equiv)


def solution(mesh):
    return jax.shard_map(
        body,
        mesh=mesh,
        in_specs=(
            P(None, None, None, "gy", "gx"),
            P(None, None, "gy", "gx"),
            P(None, "gy", "gx"),
            P(None, "gy", "gx"),
            P("gy", "gx"),
            P("gx", None),
            P("gx", None),
            P(),
            P(("gx", "gy"), None),
            P(("gx", "gy")),
            P(None, ("gx", "gy")),
            P(("gx", "gy")),
        ),
        out_specs=(
            P(None, None, None, "gy", "gx"),
            P(None, "gy", "gx"),
            P(None, None, ("gx", "gy")),
        ),
        check_vma=False,
    )
```

profile of v0, /device:TPU:1, one launch (start us, length us, event | category | flops | bytes accessed | tf_op | source)
XLA Modules:
  0.0 489.2 jit_solution(15231277766906948029)
XLA Ops:
  9.6 51.3 %all-gather.4.cloned.1.call-done = f32[12,48,3072]{2,1,0:T(8,128)} async-done(((f32[12,48,384]{2,1,0:T(8,128)}), f32[12,48,3072]{2,1,0:T(8,128)}) %all-gather.4.cloned.1.call-update) | async-done | bytes 7077904 | tf_op jit(solution)/shard_map/all_gather | solution.py:55
  60.9 15.1 %fusion.11 = f32[12,384,48]{1,2,0:T(8,128)} fusion(f32[12,48,3072]{2,1,0:T(8,128)} %all-gather.4.cloned.1.call-done, f32[384,3072]{1,0:T(8,128)} %param.17, f32[384,48]{0,1:T(8,128)S(1)} %get-tuple-element.41), kind=kOutput, calls=%fused_computation.16 | convolution fusion | flops 8153948160 | bytes 12754944 | tf_op jit(solution)/shard_map/fyb,ab->fya/dot_general | solution.py:53
  78.4 3.3 reshape.729
  81.7 42.5 %all_to_all.82 = f32[32,1,6912]{2,1,0:T(1,128)S(1)} all-to-all(f32[32,1,6912]{2,1,0:T(1,128)} %reshape.729), channel_id=1, replica_groups=mesh['gx'=8,'gy'=32] {'gy'}, dimensions={0} | all-to-all | bytes 1769472 | tf_op jit(solution)/shard_map/all_to_all | solution.py:60
  124.7 3.8 reduce.1
  134.2 3.1 all_to_all.61
  137.4 12.0 %fusion.2 = f32[12,12,1536]{2,1,0:T(8,128)S(1)} fusion(f32[12,12,1536]{2,1,0:T(8,128)S(1)} %all_to_all.61, f32[1536,1536]{1,0:T(8,128)} %all-gather.6.cloned.1.call-done), kind=kOutput, calls=%fused_computation.7 | convolution fusion | flops 4076863488 | bytes 11206656 | tf_op jit(solution)/shard_map/fxb,ab->fxa/dot_general | solution.py:61
  149.4 8.6 %copy.95 = f32[12,12,1536]{1,0,2:T(8,128)} copy(f32[12,12,1536]{2,1,0:T(8,128)S(1)} %fusion.2) | data formatting | bytes 1769472 | tf_op jit(solution)/shard_map/fxb,ab->fxa/dot_general | solution.py:61
  158.0 10.0 %reshape.731 = f32[32,1,6912]{2,1,0:T(1,128)} reshape(f32[1536,12,12]{2,1,0:T(8,128)} %bitcast.172) | data formatting | bytes 1769472
  168.0 8.0 %all-to-all-start.1 = ((f32[32,1,6912]{2,1,0:T(1,128)}), f32[32,1,6912]{2,1,0:T(1,128)S(1)}, u32[]{:S(2)}, u32[]{:S(2)}) async-start(f32[32,1,6912]{2,1,0:T(1,128)} %reshape.731), calls=%async_computation.1 | async-start | bytes 1769472 | tf_op jit(solution)/shard_map/all_to_all | solution.py:62
  180.4 17.1 %all-to-all-done.1 = f32[32,1,6912]{2,1,0:T(1,128)S(1)} async-done(((f32[32,1,6912]{2,1,0:T(1,128)}), f32[32,1,6912]{2,1,0:T(1,128)S(1)}, u32[]{:S(2)}, u32[]{:S(2)}) %all-to-all-start.1) | async-done | bytes 884768 | tf_op jit(solution)/shard_map/all_to_all | solution.py:62
  200.2 8.0 %reshape.732 = f32[1536,12,12]{2,1,0:T(8,128)} reshape(f32[32,6912]{1,0:T(8,128)S(1)} %reduce.2) | data formatting | bytes 1769472
  208.2 9.7 %copy.96 = f32[12,12,32,48]{3,1,2,0:T(8,128)S(1)} copy(f32[12,12,32,48]{1,0,3,2:T(8,128)} %bitcast.174) | data formatting | bytes 1769472 | tf_op jit(solution)/shard_map/all_to_all | solution.py:62
  225.6 46.7 %all-gather.8.cloned.1.call-done = f32[12,48,3072]{2,1,0:T(8,128)} async-done(((f32[12,48,384]{2,1,0:T(8,128)}), f32[12,48,3072]{2,1,0:T(8,128)}) %all-gather.8.cloned.1.call-update) | async-done | bytes 7077904 | tf_op jit(solution)/shard_map/all_gather | solution.py:55
  272.4 15.1 %fusion.17 = f32[12,384,48]{1,2,0:T(8,128)} fusion(f32[12,48,3072]{2,1,0:T(8,128)} %all-gather.8.cloned.1.call-done, f32[384,3072]{1,0:T(8,128)} %param.17, f32[384,48]{0,1:T(8,128)S(1)} %copy-done.8), kind=kOutput, calls=%fused_computation.18 | convolution fusion | flops 8153948160 | bytes 12754944 | tf_op jit(solution)/shard_map/fyb,ab->fya/dot_general | solution.py:53
  289.8 3.3 reshape.733
  293.1 9.7 %all-to-all-start.2 = ((f32[32,1,6912]{2,1,0:T(1,128)}), f32[32,1,6912]{2,1,0:T(1,128)S(1)}, u32[]{:S(2)}, u32[]{:S(2)}) async-start(f32[32,1,6912]{2,1,0:T(1,128)} %reshape.733), calls=%async_computation.2 | async-start | bytes 1769472 | tf_op jit(solution)/shard_map/all_to_all | solution.py:60
  303.9 20.3 %all-to-all-done.2 = f32[32,1,6912]{2,1,0:T(1,128)S(1)} async-done(((f32[32,1,6912]{2,1,0:T(1,128)}), f32[32,1,6912]{2,1,0:T(1,128)S(1)}, u32[]{:S(2)}, u32[]{:S(2)}) %all-to-all-start.2) | async-done | bytes 884768 | tf_op jit(solution)/shard_map/all_to_all | solution.py:60
  324.2 3.8 reduce.3
  333.7 3.1 all_to_all.69
  336.8 12.0 %fusion = f32[12,12,1536]{2,1,0:T(8,128)S(1)} fusion(f32[12,12,1536]{2,1,0:T(8,128)S(1)} %all_to_all.69, f32[1536,1536]{1,0:T(8,128)} %all-gather.6.cloned.1.call-done), kind=kOutput, calls=%fused_computation.5 | convolution fusion | flops 4076863488 | bytes 11206656 | tf_op jit(solution)/shard_map/fxb,ab->fxa/dot_general | solution.py:61
  348.8 8.8 %copy.101 = f32[12,12,1536]{1,0,2:T(8,128)} copy(f32[12,12,1536]{2,1,0:T(8,128)S(1)} %fusion) | data formatting | bytes 1769472 | tf_op jit(solution)/shard_map/fxb,ab->fxa/dot_general | solution.py:61
  357.7 10.0 %reshape.735 = f32[32,1,6912]{2,1,0:T(1,128)} reshape(f32[1536,12,12]{2,1,0:T(8,128)} %bitcast.173) | data formatting | bytes 1769472
  367.7 8.4 %all-to-all-start.3 = ((f32[32,1,6912]{2,1,0:T(1,128)}), f32[32,1,6912]{2,1,0:T(1,128)S(1)}, u32[]{:S(2)}, u32[]{:S(2)}) async-start(f32[32,1,6912]{2,1,0:T(1,128)} %reshape.735), calls=%async_computation.3 | async-start | bytes 1769472 | tf_op jit(solution)/shard_map/all_to_all | solution.py:62
  376.5 21.0 %all-to-all-done.3 = f32[32,1,6912]{2,1,0:T(1,128)S(1)} async-done(((f32[32,1,6912]{2,1,0:T(1,128)}), f32[32,1,6912]{2,1,0:T(1,128)S(1)}, u32[]{:S(2)}, u32[]{:S(2)}) %all-to-all-start.3) | async-done | bytes 884768 | tf_op jit(solution)/shard_map/all_to_all | solution.py:62
  400.3 7.6 %reshape.736 = f32[1536,12,12]{2,1,0:T(8,128)} reshape(f32[32,6912]{1,0:T(8,128)S(1)} %reduce.4) | data formatting | bytes 1769472
  407.9 9.7 %copy.102 = f32[12,12,32,48]{3,1,2,0:T(8,128)S(1)} copy(f32[12,12,32,48]{1,0,3,2:T(8,128)} %bitcast.175) | data formatting | bytes 1769472 | tf_op jit(solution)/shard_map/all_to_all | solution.py:62
  424.9 5.7 %copy.106 = f32[1,13,48,384]{1,3,2,0:T(8,128)} copy(f32[1,13,48,384]{3,2,1,0:T(8,128)S(1)} %pad_maximum_fusion) | data formatting | bytes 1916928 | tf_op jit(solution)/shard_map/concatenate | solution.py:75
  440.4 12.1 %scatter_fusion = f32[2,13,256]{1,2,0:T(8,128)S(1)} fusion(f32[2,13,256]{1,2,0:T(8,128)S(1)} %broadcast_in_dim.15, s32[256]{0:T(256)S(1)} %bitcast.176, f32[256,13]{1,0:T(8,128)S(1)} %copy.111), kind=kCustom, calls=%fused_computation.4 | custom fusion | bytes 41984 | tf_op jit(solution)/shard_map/scatter | solution.py:103
  452.8 12.6 %all_to_all.83 = f32[8,1,832]{2,1,0:T(1,128)S(1)} all-to-all(f32[8,1,832]{2,1,0:T(1,128)S(1)} %reshape.737), channel_id=1, replica_groups=mesh['gx'=8,'gy'=32] {'gx'}, dimensions={0} | all-to-all | bytes 53248 | tf_op jit(solution)/shard_map/all_to_all | solution.py:107
  467.3 4.4 all-to-all-start.5
  472.7 7.8 %all-to-all-done.5 = f32[32,1,208]{2,1,0:T(1,128)S(1)} async-done(((f32[32,1,208]{2,1,0:T(1,128)}), f32[32,1,208]{2,1,0:T(1,128)S(1)}, u32[]{:S(2)}, u32[]{:S(2)}) %all-to-all-start.5) | async-done | bytes 26656 | tf_op jit(solution)/shard_map/all_to_all | solution.py:106
  (113 shorter events, 59.1 us)
Async XLA Ops:
  7.2 53.7 %all-gather.4.cloned.1.call-start = ((), (), s32[]{:S(2)}) async-start(), calls=%async_computation.6 | async-start | bytes 7962624 | tf_op jit(solution)/shard_map/all_gather | solution.py:55
  7.9 129.5 %all-gather.6.cloned.1.call-start = ((), (), s32[]{:S(2)}) async-start(), calls=%async_computation.7 | async-start | bytes 10616832 | tf_op jit(solution)/shard_map/all_gather | solution.py:51
  9.5 51.3 %copy-start.7 = (f32[384,48]{0,1:T(8,128)}, f32[384,48]{0,1:T(8,128)S(1)}, u32[]{:S(2)}) copy-start(f32[384,48]{0,1:T(8,128)S(1)} %get-tuple-element.41) | copy-start | bytes 221188
  158.0 18.9 %copy-start = (f32[5,48,384]{2,1,0:T(8,128)S(1)}, f32[5,48,384]{2,1,0:T(8,128)}, u32[]{:S(2)}) copy-start(f32[5,48,384]{2,1,0:T(8,128)} %param.14) | copy-start | bytes 1105924
  168.0 29.5 %all-to-all-start.1 = ((f32[32,1,6912]{2,1,0:T(1,128)}), f32[32,1,6912]{2,1,0:T(1,128)S(1)}, u32[]{:S(2)}, u32[]{:S(2)}) async-start(f32[32,1,6912]{2,1,0:T(1,128)} %reshape.731), calls=%async_computation.1 | async-start | bytes 1769472 | tf_op jit(solution)/shard_map/all_to_all | solution.py:62
  176.0 96.3 %all-gather.8.cloned.1.call-start = ((), (), s32[]{:S(2)}) async-start(), calls=%async_computation.8 | async-start | bytes 7962624 | tf_op jit(solution)/shard_map/all_gather | solution.py:55
  177.6 2.8 copy-start.3
  178.3 0.6 copy-start.2
  222.2 50.2 %copy-start.8 = (f32[384,48]{0,1:T(8,128)S(1)}, f32[384,48]{0,1:T(8,128)}, u32[]{:S(2)}) copy-start(f32[384,48]{0,1:T(8,128)} %copy-done.7) | copy-start | bytes 221188
  224.7 0.9 copy-start.1
  287.5 16.0 %copy-start.11 = (s32[256,1]{0,1:T(1,128)S(1)}, s32[256,1]{0,1:T(1,128)}, u32[]{:S(2)}) copy-start(s32[256,1]{0,1:T(1,128)} %param.20) | copy-start | bytes 3076
  293.1 31.1 %all-to-all-start.2 = ((f32[32,1,6912]{2,1,0:T(1,128)}), f32[32,1,6912]{2,1,0:T(1,128)S(1)}, u32[]{:S(2)}, u32[]{:S(2)}) async-start(f32[32,1,6912]{2,1,0:T(1,128)} %reshape.733), calls=%async_computation.2 | async-start | bytes 1769472 | tf_op jit(solution)/shard_map/all_to_all | solution.py:60
  303.8 20.4 %copy-start.4 = (s32[256,2,128]{0,1,2:T(2,128)}, s32[256,2,128]{0,1,2:T(2,128)S(1)}, u32[]{:S(2)}) copy-start(s32[256,2,128]{0,1,2:T(2,128)S(1)} %fusion.23) | copy-start | bytes 786436
  303.9 29.8 %copy-start.12 = (s32[256,3]{0,1:T(4,128)}, s32[256,3]{0,1:T(4,128)S(1)}, u32[]{:S(2)}) copy-start(s32[256,3]{0,1:T(4,128)S(1)} %reduce-window.9) | copy-start | bytes 9220
  357.7 18.4 %slice-start = ((s32[256,3]{0,1:T(4,128)}), s32[256,2]{0,1:T(2,128)S(1)}, s32[]{:S(2)}) async-start(s32[256,3]{0,1:T(4,128)} %copy-done.12), calls=%async_computation.9 | async-start | bytes 4096 | tf_op jit(solution)/shard_map/slice.1
  357.7 18.4 %copy-start.5 = (s32[256,2,128]{0,1,2:T(2,128)S(1)}, s32[256,2,128]{0,1,2:T(2,128)}, u32[]{:S(2)}) copy-start(s32[256,2,128]{0,1,2:T(2,128)} %copy-done.4) | copy-start | bytes 786436
  357.7 18.7 %copy-start.15 = (f32[2,6]{1,0:T(2,128)S(1)}, f32[2,6]{1,0:T(2,128)}, u32[]{:S(2)}) copy-start(f32[2,6]{1,0:T(2,128)} %param.19) | copy-start | bytes 148
  357.7 18.7 %copy-start.13 = (s32[256]{0:T(256)S(1)}, s32[256]{0:T(256)}, u32[]{:S(2)}) copy-start(s32[256]{0:T(256)} %param.21) | copy-start | bytes 3076
  357.7 18.7 %copy-start.14 = (f32[2,256]{1,0:T(2,128)S(1)}, f32[2,256]{1,0:T(2,128)}, u32[]{:S(2)}) copy-start(f32[2,256]{1,0:T(2,128)} %param.22) | copy-start | bytes 6148
  367.7 29.8 %all-to-all-start.3 = ((f32[32,1,6912]{2,1,0:T(1,128)}), f32[32,1,6912]{2,1,0:T(1,128)S(1)}, u32[]{:S(2)}, u32[]{:S(2)}) async-start(f32[32,1,6912]{2,1,0:T(1,128)} %reshape.735), calls=%async_computation.3 | async-start | bytes 1769472 | tf_op jit(solution)/shard_map/all_to_all | solution.py:62
  421.9 2.6 copy-start.6
  421.9 2.6 copy-start.9
  424.8 5.8 %copy-start.10 = (f32[48,384]{1,0:T(8,128)}, f32[48,384]{1,0:T(8,128)S(1)}, u32[]{:S(2)}) copy-start(f32[48,384]{1,0:T(8,128)S(1)} %get-tuple-element.11) | copy-start | bytes 221188
  467.3 13.2 %all-to-all-start.5 = ((f32[32,1,208]{2,1,0:T(1,128)}), f32[32,1,208]{2,1,0:T(1,128)S(1)}, u32[]{:S(2)}, u32[]{:S(2)}) async-start(f32[32,1,208]{2,1,0:T(1,128)} %reshape.739), calls=%async_computation.5 | async-start | bytes 65536 | tf_op jit(solution)/shard_map/all_to_all | solution.py:106
Sparse Core Ops, SparseCore 0:
  9.8 51.0 all-gather.3
  62.7 56.8 all-gather.5
  225.8 46.5 all-gather.7
where the time goes:
time: 498 us; the launch traced here: 489 us
  waiting for transfers between devices  166 us (33%)
  local copies, waits for them, and re-layouts  140 us (28%)
  blocking collectives  55.2 us (11%)
  matrix products  54.3 us (11%)
  starting transfers between devices  30.6 us (6%)
  other arithmetic  28 us (6%)
  between operations  15.3 us (3%)
    all_gather x2, waiting for transfers between devices, body(): lax.all_gather(grid_field, 'gx', axis=2, tiled=True)  98 us
    unnamed x49, local copies, waits for them, and re-layouts  50.9 us
    all_to_all x1, blocking collectives, body(): lax.all_to_all(turned, 'gy', split_axis=1, concat_axis=2, tiled=True)  42.5 us
    all_to_all x2, waiting for transfers between devices, body(): lax.all_to_all(solved, 'gy', split_axis=2, concat_axis=1, tiled=True)  38.1 us
    dot_general x2, matrix products, body(): jnp.einsum('fyb,ab->fya', lax.all_gather(grid_field, 'gx', axis=2, tiled=...  30.3 us
    dot_general x2, matrix products, body(): solved = jnp.einsum('fxb,ab->fxa', merid_lines, whole_y, precision=highest)  24 us
    all_to_all x4, local copies, waits for them, and re-layouts, body(): lax.all_to_all(solved, 'gy', split_axis=2, concat_axis=1, tiled=True)  22.5 us
    all_to_all x1, waiting for transfers between devices, body(): lax.all_to_all(turned, 'gy', split_axis=1, concat_axis=2, tiled=True)  20.3 us
  transfers between devices with their start and end apart: 7, of which 6 were waited for; matrix products, arithmetic and copies ran while one was open for 8% of the time, Pallas kernels for 0%

commit v1 on v0

v1 whole, which is shorter than its diff:
```python
import functools

import jax
import jax.numpy as jnp
from jax import lax
from jax.experimental import pallas as pl
from jax.experimental.pallas import tpu as pltpu
from jax.sharding import PartitionSpec as P

F32, BF16, I32 = jnp.float32, jnp.bfloat16, jnp.int32
MESH = pl.DeviceIdType.MESH
ANY = pl.ANY

STEPS, KINDS, LEV = 2, 2, 6
ROWS, COLS, LANES = 48, 384, 128
LB = COLS // LANES
UNITS = LEV * LB
YR, NX, NZ = 4, 4, 8
GX, GY = 2 * YR, NX * NZ
NLAT, NLON = GY * ROWS, GX * COLS
YSH = NLAT // GX
YSB = YSH // NX
SLOTS, CAP, REC, DEV = 256, 2, 13, GX * GY
HALF = LEV // 2


def split2(v):
    hi = v.astype(BF16)
    lo = (v - hi.astype(F32)).astype(BF16)
    return hi, lo


def kernel(
    ctrl,
    sigma,
    kappa,
    beta,
    sea,
    xinv,
    yinv,
    ssh,
    owner,
    tidx,
    frac,
    count,
    inc,
    height,
    obs,
    G,
    XT,
    xbuf,
    Yf,
    Yhi,
    Ylo,
    U,
    R,
    xout,
    yout,
    F,
    acc,
    W,
    cs,
    rp,
    sig_v,
    kap_v,
    bet_v,
    sea_v,
    wx,
    wy,
    ob_i,
    ob_o,
    ob_a,
    ob_m,
    ob_f,
    own_sem,
    in_sem,
    xs_send,
    xs_recv,
    ys_send,
    ys_recv,
    yx_send,
    yx_recv,
    yb_send,
    yb_recv,
    a_send,
    a_recv,
    r_send,
    r_recv,
    o_send,
    o_recv,
):
    gx, gy = lax.axis_index("gx"), lax.axis_index("gy")
    y, c = gx // 2, gx % 2
    x, z = gy // NZ, gy % NZ
    yp, ym, yo = (y + 1) % YR, (y + YR - 1) % YR, (y + 2) % YR
    sib = (2 * y + 1 - c, gy)

    def col(yy):
        return (2 * yy + c, gy)

    def rcopy(src, dst, ssem, rsem, dev):
        return pltpu.make_async_remote_copy(
            src_ref=src, dst_ref=dst, send_sem=ssem, recv_sem=rsem, device_id=dev, device_id_type=MESH
        )

    def wait(ref, sem):
        pltpu.make_async_copy(ref, ref, sem).wait()

    def worker(kind, u):
        q = (18 * kind + 18 * c + u) % GY
        wx_ = q % NX
        return wx_ * NZ + (q // NX + 2 * wx_) % NZ

    def my_unit(kind):
        q = ((z + 2 * NZ - 2 * x) % NZ) * NX + x
        return (q + 4 * GY - 18 * kind - 18 * c) % GY

    loads = [
        pltpu.make_async_copy(xinv, xbuf, in_sem.at[0]),
        pltpu.make_async_copy(kappa, kap_v, in_sem.at[1]),
        pltpu.make_async_copy(sea, sea_v, in_sem.at[2]),
        pltpu.make_async_copy(sigma, sig_v, in_sem.at[3]),
        pltpu.make_async_copy(beta, bet_v, in_sem.at[4]),
        pltpu.make_async_copy(yinv, Yf.at[pl.ds(gx * YSH, YSH)], in_sem.at[5]),
    ]
    for load in loads[:3]:
        load.start()

    barrier = pltpu.get_barrier_semaphore()
    for i in range(1, GX):
        pl.semaphore_signal(barrier, inc=1, device_id=((gx + i) % GX, gy), device_id_type=MESH)

    @pl.loop(1, GY)
    def _(i):
        pl.semaphore_signal(barrier, inc=1, device_id=(gx, (gy + i) % GY), device_id_type=MESH)

    pl.semaphore_wait(barrier, GX + GY - 2)

    def tile_src(s, k):
        return ctrl.at[k] if s == 0 else F.at[k]

    def x_own_sends(s, k):
        src = tile_src(s, k)
        dst = G.at[s, k, y, c]
        rcopy(src, dst, xs_send.at[s, k, 0], xs_recv.at[s, k, 0], col(yp)).start()
        rcopy(src, dst, xs_send.at[s, k, 1], xs_recv.at[s, k, 1], col(ym)).start()
        rcopy(src, dst, xs_send.at[s, k, 2], xs_recv.at[s, k, 2], sib).start()
        pltpu.make_async_copy(src, dst, own_sem.at[s, k]).start()

    def x_pass(s, k, i):
        piece = G.at[s, k, ym if i == 0 else yp, c]
        wait(piece, xs_recv.at[s, k, i])
        part = piece.at[pl.ds(i * HALF, HALF)]
        rcopy(part, part, xs_send.at[s, k, 3 + i], xs_recv.at[s, k, 3 + i], col(yp if i == 0 else ym)).start()
        rcopy(piece, piece, xs_send.at[s, k, 5 + i], xs_recv.at[s, k, 5 + i], sib).start()

    def x_pass_far(s, k, i):
        part = G.at[s, k, yo, c, pl.ds(i * HALF, HALF)]
        wait(part, xs_recv.at[s, k, 3 + i])
        rcopy(part, part, xs_send.at[s, k, 7 + i], xs_recv.at[s, k, 7 + i], sib).start()

    def x_chunk(s, k, yy, first):
        lhs = jnp.concatenate(
            [G[s, k, yy, 0].reshape(LEV * ROWS, COLS), G[s, k, yy, 1].reshape(LEV * ROWS, COLS)], axis=1
        )
        hi, lo = split2(lhs)
        rhs = XT[pl.ds(pl.multiple_of(yy * 2 * COLS, 2 * COLS), 2 * COLS), :]
        p = jnp.dot(hi, rhs, preferred_element_type=F32)
        q = jnp.dot(lo, rhs[:, :COLS], preferred_element_type=F32)
        val = (p[:, :COLS] + p[:, COLS:]) + q
        if first:
            acc[...] = val
        else:
            acc[...] += val

    def x_finish(s, k):
        for lb in range(LB):
            m = sea_v[:, lb * LANES : (lb + 1) * LANES].astype(F32)
            for f in range(LEV):
                xout[s, k, f * LB + lb] = m * acc[f * ROWS : (f + 1) * ROWS, lb * LANES : (lb + 1) * LANES]

        @pl.loop(0, UNITS)
        def _(u):
            g = worker(k, u)
            src = xout.at[s, k, u]
            dst = U.at[s, k, pl.ds(pl.multiple_of(gy * ROWS, ROWS), ROWS)]

            @pl.when(g != gy)
            def _():
                rcopy(src, dst, a_send.at[s, k], a_recv.at[s, k], (gx, g)).start()

            @pl.when(g == gy)
            def _():
                pltpu.make_async_copy(src, dst, a_recv.at[s, k]).start()

    def y_phase(s, k):
        unit = my_unit(k)

        @pl.when(unit < UNITS)
        def _():
            wait(U.at[s, k], a_recv.at[s, k])
            hi, lo = split2(U[s, k])
            W[:, :LANES] = hi
            W[:, LANES:] = lo

            @pl.loop(0, 4)
            def _(m):
                rows = pl.ds(pl.multiple_of(m * 8 * ROWS, 8 * ROWS), 8 * ROWS)
                p = jnp.dot(Yhi[rows, :], W[...], preferred_element_type=F32)
                q = jnp.dot(Ylo[rows, :], W[:, :LANES], preferred_element_type=F32)
                yout[s, k, rows] = (p[:, :LANES] + p[:, LANES:]) + q

                @pl.loop(0, 8)
                def _(i):
                    g = m * 8 + i
                    src = yout.at[s, k, pl.ds(pl.multiple_of(g * ROWS, ROWS), ROWS)]
                    dst = R.at[s, k, unit]

                    @pl.when(g != gy)
                    def _():
                        rcopy(src, dst, r_send.at[s, k], r_recv.at[s, k], (gx, g)).start()

                    @pl.when(g == gy)
                    def _():
                        pltpu.make_async_copy(src, dst, r_recv.at[s, k]).start()

    def solve(s, k, lb):
        sl = slice(lb * LANES, (lb + 1) * LANES)
        m = sea_v[:, sl].astype(F32)
        d = []
        for l in range(LEV):
            v = R[s, k, l * LB + lb] * m
            if l > 0:
                v = v + kap_v[l - 1, :, sl] * d[-1]
            d.append(v * rp[l, :, sl])
        u = [d[-1]]
        for l in range(LEV - 2, -1, -1):
            u.insert(0, d[l] + cs[l, :, sl] * u[0])
        return u

    def interp_rows(vals, base):
        hi, lo = split2(vals.reshape(-1, COLS))
        p = jnp.dot(hi, wx[...], preferred_element_type=F32)
        q = jnp.dot(lo, wx[:, :SLOTS], preferred_element_type=F32)
        v = ((p[:, :SLOTS] + p[:, SLOTS:]) + q).reshape(-1, ROWS, SLOTS)
        for i in range(v.shape[0]):
            ob_i[pl.ds(base + i, 1), :] = jnp.sum(v[i] * wy[...], axis=0, keepdims=True)

    x_own_sends(0, 0)
    yrow = pl.multiple_of(x * YSB, YSB)

    def yblock(shard, xx, n=1):
        return Yf.at[pl.ds(pl.multiple_of(shard * YSH + xx * YSB, YSB), n * YSB)]

    for i, yy in enumerate((yp, ym, yo)):
        rcopy(yinv.at[pl.ds(yrow, YSB)], yblock(gx, x), ys_send.at[i], ys_recv.at[i], col(yy)).start()
    rcopy(yinv, yblock(gx, 0, NX), yb_send.at[0], yb_recv, sib).start()
    for load in loads[3:]:
        load.start()

    loads[1].wait()
    loads[2].wait()
    for lb in range(LB):
        sl = slice(lb * LANES, (lb + 1) * LANES)
        prev = None
        for l in range(LEV):
            diag = 1.0
            if l > 0:
                diag = diag + kap_v[l - 1, :, sl]
            if l < LEV - 1:
                diag = diag + kap_v[l, :, sl]
            pivot = diag if l == 0 else diag - kap_v[l - 1, :, sl] * prev
            rec = 1.0 / pivot
            rp[l, :, sl] = rec
            if l < LEV - 1:
                prev = kap_v[l, :, sl] * rec
                cs[l, :, sl] = prev

    loads[0].wait()

    @pl.loop(0, NLON // 256)
    def _(j):
        at = pl.ds(pl.multiple_of(j * 256, 256), 256)
        hi, lo = split2(xbuf[:, at].T)
        XT[at, :COLS] = hi
        XT[at, COLS:] = lo

    def x_phase(s, k, after_pass, before_end):
        wait(G.at[s, k, y, c], own_sem.at[s, k])
        wait(G.at[s, k, y, 1 - c], xs_recv.at[s, k, 2])
        x_chunk(s, k, y, True)
        x_pass(s, k, 0)
        x_pass(s, k, 1)
        after_pass()
        wait(G.at[s, k, ym, 1 - c], xs_recv.at[s, k, 5])
        x_chunk(s, k, ym, False)
        wait(G.at[s, k, yp, 1 - c], xs_recv.at[s, k, 6])
        x_chunk(s, k, yp, False)
        before_end()
        x_pass_far(s, k, 0)
        x_pass_far(s, k, 1)
        for i in range(2):
            wait(G.at[s, k, yo, 1 - c, pl.ds(i * HALF, HALF)], xs_recv.at[s, k, 7 + i])
        x_chunk(s, k, yo, False)
        x_finish(s, k)

    def y_first():
        x_own_sends(0, 1)
        for i, yy in enumerate((ym, yp, yo)):
            block = yblock(2 * yy + c, x)
            wait(block, ys_recv.at[i])
            for j in range(1, NX):
                rcopy(block, block, yx_send, yx_recv.at[i], (gx, ((x + j) % NX) * NZ + z)).start()
            rcopy(block, block, yb_send.at[1 + i], yb_recv, sib).start()

    def y_second():
        for i, yy in enumerate((ym, yp, yo)):
            wait(Yf.at[pl.ds(0, 3 * YSB)], yx_recv.at[i])
            for j in range(1, NX):
                block = yblock(2 * yy + c, (x + j) % NX)
                rcopy(block, block, yb_send.at[4 + 3 * i + j - 1], yb_recv, sib).start()

    def nothing():
        pass

    x_phase(0, 0, y_first, nothing)
    x_phase(0, 1, nothing, nothing)
    y_second()

    row = tidx[...]
    three = row >> 7
    trow = (three * 171) >> 9
    tcol = row - trow * COLS
    fx, fy = frac[0:1, :], frac[1:2, :]
    lon = lax.broadcasted_iota(I32, (COLS, SLOTS), 0)
    whi, wlo = split2(jnp.where(lon == tcol, 1.0 - fx, jnp.where(lon == tcol + 1, fx, 0.0)))
    wx[:, :SLOTS] = whi
    wx[:, SLOTS:] = wlo
    lat = lax.broadcasted_iota(I32, (ROWS, SLOTS), 0)
    wy[...] = jnp.where(lat == trow, 1.0 - fy, jnp.where(lat == trow + 1, fy, 0.0))

    loads[5].wait()
    wait(Yf.at[pl.ds(0, 4 * YSH)], yb_recv)

    @pl.loop(0, 8)
    def _(j):
        rows = pl.ds(pl.multiple_of(j * YSH, YSH), YSH)
        hi, lo = split2(Yf[rows, :])
        Yhi[rows, :] = hi
        Ylo[rows, :] = lo

    y_phase(0, 0)
    y_phase(0, 1)

    for k in range(KINDS):
        wait(R.at[0, k], r_recv.at[0, k])
        for lb in range(LB):
            u = solve(0, k, lb)
            for l in range(LEV):
                F[k, l, :, lb * LANES : (lb + 1) * LANES] = u[l]
        x_own_sends(1, k)

    x_phase(1, 0, nothing, nothing)
    x_phase(1, 1, nothing, nothing)
    y_phase(1, 0)
    y_phase(1, 1)

    loads[3].wait()
    loads[4].wait()
    wait(R.at[1, 0], r_recv.at[1, 0])
    for lb in range(LB):
        sl = slice(lb * LANES, (lb + 1) * LANES)
        u = solve(1, 0, lb)
        for l in range(LEV):
            inc[0, l, :, sl] = sig_v[0, l, :, sl] * u[l]
    ob_i[...] = jnp.zeros_like(ob_i)
    interp_rows(inc[0], 0)
    wait(R.at[1, 1], r_recv.at[1, 1])
    for lb in range(LB):
        sl = slice(lb * LANES, (lb + 1) * LANES)
        u = solve(1, 1, lb)
        h = None
        for l in range(LEV):
            t = inc[0, l, :, sl]
            v = sig_v[1, l, :, sl] * u[l] + bet_v[l, :, sl] * t
            inc[1, l, :, sl] = v
            term = ssh[0, l] * t + ssh[1, l] * v
            h = term if h is None else h + term
        height[:, sl] = h
    interp_rows(inc[1], LEV)
    interp_rows(height[...], 2 * LEV)

    own_row = owner[...]
    ia = lax.broadcasted_iota(I32, (SLOTS, SLOTS), 0)
    ib = lax.broadcasted_iota(I32, (SLOTS, SLOTS), 1)
    own_f = own_row.astype(F32)
    own_col = jnp.sum(jnp.where(ia == ib, own_f, 0.0), axis=1, keepdims=True)
    earlier = jnp.where((own_col == own_f) & (ia < ib), 1.0, 0.0)
    rank = jnp.sum(earlier, axis=0, keepdims=True)
    live = lax.broadcasted_iota(I32, (1, SLOTS), 1) < count[0]
    values = jnp.where(live, ob_i[...], 0.0)
    placed = jnp.concatenate(
        [
            jnp.where(rank == 0.0, values, 0.0),
            jnp.where(rank == 1.0, values, 0.0),
            jnp.zeros((LANES - 32, SLOTS), F32),
        ],
        axis=0,
    )
    target = (own_row % GY) * GX + own_row // GY
    pick = jnp.where(ia == target, 1.0, 0.0).astype(BF16)
    hi, mid = split2(placed)
    low = ((placed - hi.astype(F32)) - mid.astype(F32)).astype(BF16)
    dims = (((1,), (1,)), ((), ()))
    ob_o[...] = (
        lax.dot_general(pick, hi, dims, preferred_element_type=F32)
        + lax.dot_general(pick, mid, dims, preferred_element_type=F32)
    ) + lax.dot_general(pick, low, dims, preferred_element_type=F32)

    @pl.loop(0, GY)
    def _(g):
        src = ob_o.at[pl.ds(pl.multiple_of(g * GX, GX), GX)]
        dst = ob_a.at[pl.ds(pl.multiple_of(gy * GX, GX), GX)]

        @pl.when(g != gy)
        def _():
            rcopy(src, dst, o_send.at[0], o_recv.at[0], (gx, g)).start()

        @pl.when(g == gy)
        def _():
            pltpu.make_async_copy(src, dst, o_recv.at[0]).start()

    wait(ob_a, o_recv.at[0])
    for g in range(GX):
        ob_m[g] = ob_a[pl.ds(g, GY, stride=GX), :]
    for g in range(GX):
        src = ob_m.at[g]
        dst = ob_f.at[pl.ds(pl.multiple_of(gx * GY, GY), GY)]

        @pl.when(g != gx)
        def _():
            rcopy(src, dst, o_send.at[1], o_recv.at[1], (g, gy)).start()

        @pl.when(g == gx)
        def _():
            pltpu.make_async_copy(src, dst, o_recv.at[1]).start()

    wait(ob_f, o_recv.at[1])
    turned = ob_f[...].T
    obs[0] = turned[0:REC]
    obs[1] = turned[16 : 16 + REC]

    for s in range(STEPS):
        for k in range(KINDS):
            whole = G.at[s, k, y, c]
            half = G.at[s, k, y, c, pl.ds(0, HALF)]
            for i in range(9):
                wait(half if i in (3, 4, 7, 8) else whole, xs_send.at[s, k, i])
            mine = my_unit(k) < UNITS

            @pl.when(mine)
            def _():
                wait(xout.at[s, k, pl.ds(0, UNITS - 1)], a_send.at[s, k])
                wait(yout.at[s, k, pl.ds(0, (GY - 1) * ROWS)], r_send.at[s, k])

            @pl.when(jnp.logical_not(mine))
            def _():
                wait(xout.at[s, k], a_send.at[s, k])

    for i in range(3):
        wait(yblock(0, 0), ys_send.at[i])
    wait(yblock(0, 0, 9), yx_send)
    wait(yblock(0, 0, NX), yb_send.at[0])
    for i in range(12):
        wait(yblock(0, 0), yb_send.at[1 + i])
    wait(ob_o.at[pl.ds(0, (GY - 1) * GX)], o_send.at[0])
    wait(ob_m.at[pl.ds(0, GX - 1)], o_send.at[1])


def body(
    control, sigma, kappa, beta, sea_mask, x_inverse, y_inverse, ssh_coef, obs_owner, tile_index, obs_frac, obs_count
):
    vmem = pl.BlockSpec(memory_space=pltpu.VMEM)
    smem = pl.BlockSpec(memory_space=pltpu.SMEM)
    hbm = pl.BlockSpec(memory_space=ANY)
    dma = pltpu.SemaphoreType.DMA
    tile = (ROWS, COLS)
    inc, height, obs = pl.pallas_call(
        kernel,
        out_shape=(
            jax.ShapeDtypeStruct((KINDS, LEV) + tile, F32),
            jax.ShapeDtypeStruct(tile, F32),
            jax.ShapeDtypeStruct((CAP, REC, DEV), F32),
        ),
        in_specs=[hbm] * 7 + [smem, vmem, vmem, vmem, smem],
        out_specs=(vmem, vmem, vmem),
        scratch_shapes=[
            pltpu.VMEM((STEPS, KINDS, YR, 2, LEV) + tile, F32),
            pltpu.VMEM((NLON, 2 * COLS), BF16),
            pltpu.VMEM((COLS, NLON), F32),
            pltpu.VMEM((NLAT, NLAT), F32),
            pltpu.VMEM((NLAT, NLAT), BF16),
            pltpu.VMEM((NLAT, NLAT), BF16),
            pltpu.VMEM((STEPS, KINDS, NLAT, LANES), F32),
            pltpu.VMEM((STEPS, KINDS, UNITS, ROWS, LANES), F32),
            pltpu.VMEM((STEPS, KINDS, UNITS, ROWS, LANES), F32),
            pltpu.VMEM((STEPS, KINDS, NLAT, LANES), F32),
            pltpu.VMEM((KINDS, LEV) + tile, F32),
            pltpu.VMEM((LEV * ROWS, COLS), F32),
            pltpu.VMEM((NLAT, 2 * LANES), BF16),
            pltpu.VMEM((LEV - 1,) + tile, F32),
            pltpu.VMEM((LEV,) + tile, F32),
            pltpu.VMEM((KINDS, LEV) + tile, F32),
            pltpu.VMEM((LEV - 1,) + tile, F32),
            pltpu.VMEM((LEV,) + tile, F32),
            pltpu.VMEM(tile, I32),
            pltpu.VMEM((COLS, 2 * SLOTS), BF16),
            pltpu.VMEM((ROWS, SLOTS), F32),
            pltpu.VMEM((16, SLOTS), F32),
            pltpu.VMEM((DEV, LANES), F32),
            pltpu.VMEM((DEV, LANES), F32),
            pltpu.VMEM((GX, GY, LANES), F32),
            pltpu.VMEM((DEV, LANES), F32),
            dma((STEPS, KINDS)),
            dma((6,)),
            dma((STEPS, KINDS, 9)),
            dma((STEPS, KINDS, 9)),
            dma((3,)),
            dma((3,)),
            dma(()),
            dma((3,)),
            dma((13,)),
            dma(()),
            dma((STEPS, KINDS)),
            dma((STEPS, KINDS)),
            dma((STEPS, KINDS)),
            dma((STEPS, KINDS)),
            dma((2,)),
            dma((2,)),
        ],
        compiler_params=pltpu.CompilerParams(
            collective_id=0, has_side_effects=True, vmem_limit_bytes=62 * 1024 * 1024
        ),
        name="covariance",
    )(
        control[0],
        sigma,
        kappa,
        beta,
        sea_mask,
        x_inverse,
        y_inverse,
        ssh_coef,
        obs_owner.reshape(1, SLOTS),
        tile_index.reshape(1, SLOTS),
        obs_frac,
        obs_count,
    )
    return inc[None], height[None], obs


def solution(mesh):
    return jax.shard_map(
        body,
        mesh=mesh,
        in_specs=(
            P(None, None, None, "gy", "gx"),
            P(None, None, "gy", "gx"),
            P(None, "gy", "gx"),
            P(None, "gy", "gx"),
            P("gy", "gx"),
            P("gx", None),
            P("gx", None),
            P(),
            P(("gx", "gy"), None),
            P(("gx", "gy")),
            P(None, ("gx", "gy")),
            P(("gx", "gy")),
        ),
        out_specs=(
            P(None, None, None, "gy", "gx"),
            P(None, "gy", "gx"),
            P(None, None, ("gx", "gy")),
        ),
        check_vma=False,
    )
```

time: 498 us -> 195 us (0.39); the launches traced: 489 us -> 194 us
  Pallas kernels: 0 us -> 188 us
  waiting for transfers between devices: 166 us -> 0 us
  local copies, waits for them, and re-layouts: 140 us -> 5.04 us
  blocking collectives: 55.2 us -> 0 us
  matrix products: 54.3 us -> 0 us
  starting transfers between devices: 30.6 us -> 0 us
  other arithmetic: 28 us -> 0 us
  between operations: 15.3 us -> 1.29 us
    pallas_call x0 -> x1, Pallas kernels: none -> 188 us  [body(): pl.pallas_call(kernel, out_shape=(jax.ShapeDtypeStruct((KINDS, LEV) + til...]
    all_gather x3 -> x0, waiting for transfers between devices: 98 us -> none  [the longest x2 98 us: body(): lax.all_gather(grid_field, 'gx', axis=2, tiled=True)]
    all_to_all x4 -> x0, waiting for transfers between devices: 66.2 us -> none  [the longest x2 38.1 us: body(): lax.all_to_all(solved, 'gy', split_axis=2, concat_axis=1, tiled=True)]
    all_to_all x2 -> x0, blocking collectives: 55.2 us -> none  [the longest x1 42.5 us: body(): lax.all_to_all(turned, 'gy', split_axis=1, concat_axis=2, tiled=True)]
    dot_general x4 -> x0, matrix products: 54.3 us -> none  [the longest x2 30.3 us: body(): jnp.einsum('fyb,ab->fya', lax.all_gather(grid_field, 'gx', axis=2, tiled=...]
    unnamed x49 -> x3, local copies, waits for them, and re-layouts: 50.9 us -> 5.04 us
    all_to_all x11 -> x0, local copies, waits for them, and re-layouts: 35.3 us -> none  [the longest x4 22.5 us: body(): lax.all_to_all(solved, 'gy', split_axis=2, concat_axis=1, tiled=True)]
    all_to_all x4 -> x0, starting transfers between devices: 30.5 us -> none  [the longest x2 16.4 us: body(): lax.all_to_all(solved, 'gy', split_axis=2, concat_axis=1, tiled=True)]
  transfers between devices with their start and end apart: 7 -> 0, of which waited for: 6 -> 0; matrix products, arithmetic and copies ran while one was open for 8% -> 0% of each run, Pallas kernels for 0% -> 0%
where the time goes in v1:
time: 195 us; the launch traced here: 194 us
  Pallas kernels  188 us (96%)
  local copies, waits for them, and re-layouts  5.04 us (3%)
    pallas_call x1, Pallas kernels, body(): pl.pallas_call(kernel, out_shape=(jax.ShapeDtypeStruct((KINDS, LEV) + til...  188 us
    unnamed x3, local copies, waits for them, and re-layouts  5.04 us

profile of v1, /device:TPU:1, one launch (start us, length us, event | category | flops | bytes accessed | tf_op | source)
XLA Modules:
  0.0 194.3 jit_solution(5233814650871992808)
XLA Ops:
  1.3 187.9 %covariance.1 = (f32[2,6,48,384]{3,2,1,0:T(8,128)}, f32[48,384]{1,0:T(8,128)}, f32[2,13,256]{2,1,0:T(8,128)}) custom-call(f32[2,6,48,384]{3,2,1,0:T(8,128)} %bitcast.5, f32[2,6,48,384]{3,2,1,0:T(8,128)} %sigma.1, f32[5,48,384]{2,1,0:T(8,128)} %kappa.1, f32[6,48,384]{2,1,0:T(8,128)} %beta.1, s32[48,384]{1,0:T(8,128)} %sea.1, f32[384,3072]{1,0:T(8,128)} %xinv.1, ...), custom_call_target="tpu_custom_call" | custom-call | tf_op jit(solution)/shard_map/covariance/pallas_call | solution.py:488
  189.2 1.4 copy.15
  190.6 2.1 %copy.19 = f32[1,2,6,48,384]{4,3,2,1,0:T(8,128)} copy(f32[1,2,6,48,384]{4,3,2,1,0:T(8,128)} %bitcast.6) | data formatting | bytes 1769472
  192.7 1.5 copy.20

commit v2 on v1

--- a/solution.py
+++ b/solution.py
@@ -21,7 +21,8 @@
 YSH = NLAT // GX
 YSB = YSH // NX
 SLOTS, CAP, REC, DEV = 256, 2, 13, GX * GY
-HALF = LEV // 2
+PIECES, PLEV = 4, LEV // 2
+PUNITS = PLEV * LB
 
 
 def split2(v):
@@ -136,51 +137,70 @@
 
     pl.semaphore_wait(barrier, GX + GY - 2)
 
-    def tile_src(s, k):
-        return ctrl.at[k] if s == 0 else F.at[k]
-
-    def x_own_sends(s, k):
-        src = tile_src(s, k)
-        dst = G.at[s, k, y, c]
-        rcopy(src, dst, xs_send.at[s, k, 0], xs_recv.at[s, k, 0], col(yp)).start()
-        rcopy(src, dst, xs_send.at[s, k, 1], xs_recv.at[s, k, 1], col(ym)).start()
-        rcopy(src, dst, xs_send.at[s, k, 2], xs_recv.at[s, k, 2], sib).start()
-        pltpu.make_async_copy(src, dst, own_sem.at[s, k]).start()
-
-    def x_pass(s, k, i):
-        piece = G.at[s, k, ym if i == 0 else yp, c]
-        wait(piece, xs_recv.at[s, k, i])
-        part = piece.at[pl.ds(i * HALF, HALF)]
-        rcopy(part, part, xs_send.at[s, k, 3 + i], xs_recv.at[s, k, 3 + i], col(yp if i == 0 else ym)).start()
-        rcopy(piece, piece, xs_send.at[s, k, 5 + i], xs_recv.at[s, k, 5 + i], sib).start()
-
-    def x_pass_far(s, k, i):
-        part = G.at[s, k, yo, c, pl.ds(i * HALF, HALF)]
-        wait(part, xs_recv.at[s, k, 3 + i])
-        rcopy(part, part, xs_send.at[s, k, 7 + i], xs_recv.at[s, k, 7 + i], sib).start()
-
-    def x_chunk(s, k, yy, first):
-        lhs = jnp.concatenate(
-            [G[s, k, yy, 0].reshape(LEV * ROWS, COLS), G[s, k, yy, 1].reshape(LEV * ROWS, COLS)], axis=1
-        )
-        hi, lo = split2(lhs)
-        rhs = XT[pl.ds(pl.multiple_of(yy * 2 * COLS, 2 * COLS), 2 * COLS), :]
-        p = jnp.dot(hi, rhs, preferred_element_type=F32)
-        q = jnp.dot(lo, rhs[:, :COLS], preferred_element_type=F32)
-        val = (p[:, :COLS] + p[:, COLS:]) + q
-        if first:
-            acc[...] = val
-        else:
-            acc[...] += val
-
-    def x_finish(s, k):
+    def gat(s, p, yy, cc):
+        return G.at[s, p, yy, cc]
+
+    def half(ref, i):
+        return ref.at[:, pl.ds(i * (ROWS // 2), ROWS // 2)]
+
+    def own(s, p):
+        lev = pl.ds((p % 2) * PLEV, PLEV)
+        src = ctrl.at[p // 2, lev] if s == 0 else F.at[p // 2, lev]
+        dst = gat(s, p, y, c)
+        rcopy(src, dst, xs_send.at[s, p, 0], xs_recv.at[s, p, 0], col(yp)).start()
+        rcopy(src, dst, xs_send.at[s, p, 1], xs_recv.at[s, p, 1], col(ym)).start()
+        rcopy(src, dst, xs_send.at[s, p, 2], xs_recv.at[s, p, 2], sib).start()
+        pltpu.make_async_copy(src, dst, own_sem.at[s, p]).start()
+
+    def near(s, p):
+        for i, (yy, to) in enumerate(((ym, yp), (yp, ym))):
+            piece = gat(s, p, yy, c)
+            wait(piece, xs_recv.at[s, p, i])
+            part = half(piece, i)
+            rcopy(part, part, xs_send.at[s, p, 3 + i], xs_recv.at[s, p, 3 + i], col(to)).start()
+            rcopy(piece, piece, xs_send.at[s, p, 5 + i], xs_recv.at[s, p, 5 + i], sib).start()
+
+    def far(s, p):
+        for i in range(2):
+            part = half(gat(s, p, yo, c), i)
+            wait(part, xs_recv.at[s, p, 3 + i])
+            rcopy(part, part, xs_send.at[s, p, 7 + i], xs_recv.at[s, p, 7 + i], sib).start()
+
+    def mult(s, p):
+        wait(gat(s, p, y, c), own_sem.at[s, p])
+        wait(gat(s, p, y, 1 - c), xs_recv.at[s, p, 2])
+        wait(gat(s, p, ym, 1 - c), xs_recv.at[s, p, 5])
+        wait(gat(s, p, yp, 1 - c), xs_recv.at[s, p, 6])
+        acc[...] = jnp.zeros_like(acc)
+
+        @pl.loop(0, YR)
+        def _(t):
+            yy = (y + t * (t + 1) // 2) % YR
+
+            @pl.when(t == YR - 1)
+            def _():
+                far(s, p)
+                for i in range(2):
+                    wait(half(gat(s, p, yo, 1 - c), i), xs_recv.at[s, p, 7 + i])
+
+            lhs = jnp.concatenate([G[s, p, yy, i].reshape(PLEV * ROWS, COLS) for i in range(2)], axis=1)
+            hi, lo = split2(lhs)
+            rhs = XT[pl.ds(pl.multiple_of(yy * 2 * COLS, 2 * COLS), 2 * COLS), :]
+            pr = jnp.dot(hi, rhs, preferred_element_type=F32)
+            qr = jnp.dot(lo, rhs[:, :COLS], preferred_element_type=F32)
+            acc[...] += (pr[:, :COLS] + pr[:, COLS:]) + qr
+
+        k, first = p // 2, (p % 2) * PUNITS
         for lb in range(LB):
             m = sea_v[:, lb * LANES : (lb + 1) * LANES].astype(F32)
-            for f in range(LEV):
-                xout[s, k, f * LB + lb] = m * acc[f * ROWS : (f + 1) * ROWS, lb * LANES : (lb + 1) * LANES]
-
-        @pl.loop(0, UNITS)
-        def _(u):
+            for f in range(PLEV):
+                xout[s, k, first + f * LB + lb] = (
+                    m * acc[f * ROWS : (f + 1) * ROWS, lb * LANES : (lb + 1) * LANES]
+                )
+
+        @pl.loop(0, PUNITS)
+        def _(i):
+            u = first + (i + gy) % PUNITS
             g = worker(k, u)
             src = xout.at[s, k, u]
             dst = U.at[s, k, pl.ds(pl.multiple_of(gy * ROWS, ROWS), ROWS)]
@@ -204,7 +224,8 @@
             W[:, LANES:] = lo
 
             @pl.loop(0, 4)
-            def _(m):
+            def _(step):
+                m = (step + gy) % 4
                 rows = pl.ds(pl.multiple_of(m * 8 * ROWS, 8 * ROWS), 8 * ROWS)
                 p = jnp.dot(Yhi[rows, :], W[...], preferred_element_type=F32)
                 q = jnp.dot(Ylo[rows, :], W[:, :LANES], preferred_element_type=F32)
@@ -212,7 +233,7 @@
 
                 @pl.loop(0, 8)
                 def _(i):
-                    g = m * 8 + i
+                    g = m * 8 + (i + gy // 4) % 8
                     src = yout.at[s, k, pl.ds(pl.multiple_of(g * ROWS, ROWS), ROWS)]
                     dst = R.at[s, k, unit]
 
@@ -246,14 +267,74 @@
         for i in range(v.shape[0]):
             ob_i[pl.ds(base + i, 1), :] = jnp.sum(v[i] * wy[...], axis=0, keepdims=True)
 
-    x_own_sends(0, 0)
-    yrow = pl.multiple_of(x * YSB, YSB)
-
     def yblock(shard, xx, n=1):
         return Yf.at[pl.ds(pl.multiple_of(shard * YSH + xx * YSB, YSB), n * YSB)]
 
-    for i, yy in enumerate((yp, ym, yo)):
-        rcopy(yinv.at[pl.ds(yrow, YSB)], yblock(gx, x), ys_send.at[i], ys_recv.at[i], col(yy)).start()
+    def yhalf(shard, xx, i):
+        return Yf.at[pl.ds(pl.multiple_of(shard * YSH + xx * YSB + i * (YSB // 2), YSB // 2), YSB // 2)]
+
+    def row_dev(xx):
+        return (gx, xx * NZ + z)
+
+    def to_sib(ref, i):
+        rcopy(ref, ref, yb_send.at[i], yb_recv, sib).start()
+
+    def along_x(i, yy):
+        block = yblock(2 * yy + c, x)
+        rcopy(block, block, yx_send.at[i, 0], yx_recv.at[i, 0], row_dev(xp)).start()
+        rcopy(block, block, yx_send.at[i, 1], yx_recv.at[i, 1], row_dev(xm)).start()
+        to_sib(block, 1 + i)
+
+    def y_near():
+        for i, (yy, to) in enumerate(((ym, yp), (yp, ym))):
+            block = yblock(2 * yy + c, x)
+            wait(block, ys_recv.at[i])
+            part = yhalf(2 * yy + c, x, i)
+            rcopy(part, part, ys_send.at[2 + i], ys_recv.at[2 + i], col(to)).start()
+            along_x(i, yy)
+
+    def y_far():
+        for i in range(2):
+            wait(yhalf(2 * yo + c, x, i), ys_recv.at[2 + i])
+        along_x(2, yo)
+
+    def x_near(i):
+        yy = (ym, yp, yo)[i]
+        for j, (xx, to) in enumerate(((xm, xp), (xp, xm))):
+            block = yblock(2 * yy + c, xx)
+            wait(block, yx_recv.at[i, j])
+            part = yhalf(2 * yy + c, xx, j)
+            rcopy(part, part, yx_send.at[i, 2 + j], yx_recv.at[i, 2 + j], row_dev(to)).start()
+            to_sib(block, 4 + 4 * i + j)
+
+    def x_far(i):
+        yy = (ym, yp, yo)[i]
+        for j in range(2):
+            part = yhalf(2 * yy + c, xo, j)
+            wait(part, yx_recv.at[i, 2 + j])
+            to_sib(part, 6 + 4 * i + j)
+
+    def y_split(cc):
+        @pl.loop(0, YR)
+        def _(j):
+            rows = pl.ds(pl.multiple_of((2 * j + cc) * YSH, YSH), YSH)
+            hi, lo = split2(Yf[rows, :])
+            Yhi[rows, :] = hi
+            Ylo[rows, :] = lo
+
+    def turn(lo_, hi_):
+        @pl.loop(lo_, hi_)
+        def _(j):
+            at = pl.ds(pl.multiple_of(j * 256, 256), 256)
+            hi, lo = split2(xbuf[:, at].T)
+            XT[at, :COLS] = hi
+            XT[at, COLS:] = lo
+
+    xp, xm, xo = (x + 1) % NX, (x + NX - 1) % NX, (x + 2) % NX
+    yrow = yinv.at[pl.ds(pl.multiple_of(x * YSB, YSB), YSB)]
+    for i, yy in enumerate((yp, ym)):
+        rcopy(yrow, yblock(gx, x), ys_send.at[i], ys_recv.at[i], col(yy)).start()
+    own(0, 0)
     rcopy(yinv, yblock(gx, 0, NX), yb_send.at[0], yb_recv, sib).start()
     for load in loads[3:]:
         load.start()
@@ -277,55 +358,27 @@
                 cs[l, :, sl] = prev
 
     loads[0].wait()
-
-    @pl.loop(0, NLON // 256)
-    def _(j):
-        at = pl.ds(pl.multiple_of(j * 256, 256), 256)
-        hi, lo = split2(xbuf[:, at].T)
-        XT[at, :COLS] = hi
-        XT[at, COLS:] = lo
-
-    def x_phase(s, k, after_pass, before_end):
-        wait(G.at[s, k, y, c], own_sem.at[s, k])
-        wait(G.at[s, k, y, 1 - c], xs_recv.at[s, k, 2])
-        x_chunk(s, k, y, True)
-        x_pass(s, k, 0)
-        x_pass(s, k, 1)
-        after_pass()
-        wait(G.at[s, k, ym, 1 - c], xs_recv.at[s, k, 5])
-        x_chunk(s, k, ym, False)
-        wait(G.at[s, k, yp, 1 - c], xs_recv.at[s, k, 6])
-        x_chunk(s, k, yp, False)
-        before_end()
-        x_pass_far(s, k, 0)
-        x_pass_far(s, k, 1)
-        for i in range(2):
-            wait(G.at[s, k, yo, 1 - c, pl.ds(i * HALF, HALF)], xs_recv.at[s, k, 7 + i])
-        x_chunk(s, k, yo, False)
-        x_finish(s, k)
-
-    def y_first():
-        x_own_sends(0, 1)
-        for i, yy in enumerate((ym, yp, yo)):
-            block = yblock(2 * yy + c, x)
-            wait(block, ys_recv.at[i])
-            for j in range(1, NX):
-                rcopy(block, block, yx_send, yx_recv.at[i], (gx, ((x + j) % NX) * NZ + z)).start()
-            rcopy(block, block, yb_send.at[1 + i], yb_recv, sib).start()
-
-    def y_second():
-        for i, yy in enumerate((ym, yp, yo)):
-            wait(Yf.at[pl.ds(0, 3 * YSB)], yx_recv.at[i])
-            for j in range(1, NX):
-                block = yblock(2 * yy + c, (x + j) % NX)
-                rcopy(block, block, yb_send.at[4 + 3 * i + j - 1], yb_recv, sib).start()
-
-    def nothing():
-        pass
-
-    x_phase(0, 0, y_first, nothing)
-    x_phase(0, 1, nothing, nothing)
-    y_second()
+    turn(0, 6)
+    y_near()
+    own(0, 1)
+    turn(6, 12)
+    near(0, 0)
+    own(0, 2)
+    y_far()
+    mult(0, 0)
+    near(0, 1)
+    own(0, 3)
+    x_near(0)
+    mult(0, 1)
+    near(0, 2)
+    x_near(1)
+    x_far(0)
+    mult(0, 2)
+    near(0, 3)
+    x_near(2)
+    x_far(1)
+    mult(0, 3)
+    x_far(2)
 
     row = tidx[...]
     three = row >> 7
@@ -340,30 +393,34 @@
     wy[...] = jnp.where(lat == trow, 1.0 - fy, jnp.where(lat == trow + 1, fy, 0.0))
 
     loads[5].wait()
+    y_split(c)
     wait(Yf.at[pl.ds(0, 4 * YSH)], yb_recv)
-
-    @pl.loop(0, 8)
-    def _(j):
-        rows = pl.ds(pl.multiple_of(j * YSH, YSH), YSH)
-        hi, lo = split2(Yf[rows, :])
-        Yhi[rows, :] = hi
-        Ylo[rows, :] = lo
-
+    y_split(1 - c)
     y_phase(0, 0)
     y_phase(0, 1)
 
-    for k in range(KINDS):
+    def first_solve(k):
         wait(R.at[0, k], r_recv.at[0, k])
         for lb in range(LB):
             u = solve(0, k, lb)
             for l in range(LEV):
                 F[k, l, :, lb * LANES : (lb + 1) * LANES] = u[l]
-        x_own_sends(1, k)
-
-    x_phase(1, 0, nothing, nothing)
-    x_phase(1, 1, nothing, nothing)
+
+    first_solve(0)
+    own(1, 0)
+    own(1, 1)
+    near(1, 0)
+    first_solve(1)
+    own(1, 2)
+    mult(1, 0)
+    near(1, 1)
+    own(1, 3)
+    mult(1, 1)
+    near(1, 2)
+    mult(1, 2)
     y_phase(1, 0)
-    y_phase(1, 1)
+    near(1, 3)
+    mult(1, 3)
 
     loads[3].wait()
     loads[4].wait()
@@ -375,6 +432,7 @@
             inc[0, l, :, sl] = sig_v[0, l, :, sl] * u[l]
     ob_i[...] = jnp.zeros_like(ob_i)
     interp_rows(inc[0], 0)
+    y_phase(1, 1)
     wait(R.at[1, 1], r_recv.at[1, 1])
     for lb in range(LB):
         sl = slice(lb * LANES, (lb + 1) * LANES)
@@ -451,11 +509,11 @@
     obs[1] = turned[16 : 16 + REC]
 
     for s in range(STEPS):
+        for p in range(PIECES):
+            whole = gat(s, p, y, c)
+            for i in range(9):
+                wait(half(whole, 0) if i in (3, 4, 7, 8) else whole, xs_send.at[s, p, i])
         for k in range(KINDS):
-            whole = G.at[s, k, y, c]
-            half = G.at[s, k, y, c, pl.ds(0, HALF)]
-            for i in range(9):
-                wait(half if i in (3, 4, 7, 8) else whole, xs_send.at[s, k, i])
             mine = my_unit(k) < UNITS
 
             @pl.when(mine)
@@ -467,12 +525,14 @@
             def _():
                 wait(xout.at[s, k], a_send.at[s, k])
 
+    for i in range(4):
+        wait(yblock(0, 0) if i < 2 else yhalf(0, 0, 0), ys_send.at[i])
     for i in range(3):
-        wait(yblock(0, 0), ys_send.at[i])
-    wait(yblock(0, 0, 9), yx_send)
+        for j in range(4):
+            wait(yblock(0, 0) if j < 2 else yhalf(0, 0, 0), yx_send.at[i, j])
+            wait(yblock(0, 0) if j < 2 else yhalf(0, 0, 0), yb_send.at[4 + 4 * i + j])
+        wait(yblock(0, 0), yb_send.at[1 + i])
     wait(yblock(0, 0, NX), yb_send.at[0])
-    for i in range(12):
-        wait(yblock(0, 0), yb_send.at[1 + i])
     wait(ob_o.at[pl.ds(0, (GY - 1) * GX)], o_send.at[0])
     wait(ob_m.at[pl.ds(0, GX - 1)], o_send.at[1])
 
@@ -495,7 +555,7 @@
         in_specs=[hbm] * 7 + [smem, vmem, vmem, vmem, smem],
         out_specs=(vmem, vmem, vmem),
         scratch_shapes=[
-            pltpu.VMEM((STEPS, KINDS, YR, 2, LEV) + tile, F32),
+            pltpu.VMEM((STEPS, PIECES, YR, 2, PLEV) + tile, F32),
             pltpu.VMEM((NLON, 2 * COLS), BF16),
             pltpu.VMEM((COLS, NLON), F32),
             pltpu.VMEM((NLAT, NLAT), F32),
@@ -506,7 +566,7 @@
             pltpu.VMEM((STEPS, KINDS, UNITS, ROWS, LANES), F32),
             pltpu.VMEM((STEPS, KINDS, NLAT, LANES), F32),
             pltpu.VMEM((KINDS, LEV) + tile, F32),
-            pltpu.VMEM((LEV * ROWS, COLS), F32),
+            pltpu.VMEM((PLEV * ROWS, COLS), F32),
             pltpu.VMEM((NLAT, 2 * LANES), BF16),
             pltpu.VMEM((LEV - 1,) + tile, F32),
             pltpu.VMEM((LEV,) + tile, F32),
@@ -521,15 +581,15 @@
             pltpu.VMEM((DEV, LANES), F32),
             pltpu.VMEM((GX, GY, LANES), F32),
             pltpu.VMEM((DEV, LANES), F32),
-            dma((STEPS, KINDS)),
+            dma((STEPS, PIECES)),
             dma((6,)),
-            dma((STEPS, KINDS, 9)),
-            dma((STEPS, KINDS, 9)),
-            dma((3,)),
-            dma((3,)),
-            dma(()),
-            dma((3,)),
-            dma((13,)),
+            dma((STEPS, PIECES, 9)),
+            dma((STEPS, PIECES, 9)),
+            dma((4,)),
+            dma((4,)),
+            dma((3, 4)),
+            dma((3, 4)),
+            dma((16,)),
             dma(()),
             dma((STEPS, KINDS)),
             dma((STEPS, KINDS)),

time: 195 us -> 177 us (0.908)
  Pallas kernels: 188 us -> 170 us
    pallas_call x1, Pallas kernels: 188 us -> 170 us  [body(): pl.pallas_call(kernel, out_shape=(jax.ShapeDtypeStruct((KINDS, LEV) + til...]
where the time goes in v2:
time: 177 us; the launch traced here: 176 us
  Pallas kernels  170 us (96%)
  local copies, waits for them, and re-layouts  5.04 us (3%)
    pallas_call x1, Pallas kernels, body(): pl.pallas_call(kernel, out_shape=(jax.ShapeDtypeStruct((KINDS, LEV) + til...  170 us
    unnamed x3, local copies, waits for them, and re-layouts  5.04 us

profile of v2, /device:TPU:1, one launch (start us, length us, event | category | flops | bytes accessed | tf_op | source)
XLA Modules:
  0.0 176.0 jit_solution(5322543168881444043)
XLA Ops:
  1.3 169.7 %covariance.1 = (f32[2,6,48,384]{3,2,1,0:T(8,128)}, f32[48,384]{1,0:T(8,128)}, f32[2,13,256]{2,1,0:T(8,128)}) custom-call(f32[2,6,48,384]{3,2,1,0:T(8,128)} %bitcast.5, f32[2,6,48,384]{3,2,1,0:T(8,128)} %sigma.1, f32[5,48,384]{2,1,0:T(8,128)} %kappa.1, f32[6,48,384]{2,1,0:T(8,128)} %beta.1, s32[48,384]{1,0:T(8,128)} %sea.1, f32[384,3072]{1,0:T(8,128)} %xinv.1, ...), custom_call_target="tpu_custom_call" | custom-call | tf_op jit(solution)/shard_map/covariance/pallas_call | solution.py:548
  171.0 1.4 copy.15
  172.4 2.1 %copy.19 = f32[1,2,6,48,384]{4,3,2,1,0:T(8,128)} copy(f32[1,2,6,48,384]{4,3,2,1,0:T(8,128)} %bitcast.6) | data formatting | bytes 1769472
  174.5 1.5 copy.20

commit v3 on v2

--- a/solution.py
+++ b/solution.py
@@ -179,7 +179,6 @@
 
             @pl.when(t == YR - 1)
             def _():
-                far(s, p)
                 for i in range(2):
                     wait(half(gat(s, p, yo, 1 - c), i), xs_recv.at[s, p, 7 + i])
 
@@ -213,19 +212,22 @@
             def _():
                 pltpu.make_async_copy(src, dst, a_recv.at[s, k]).start()
 
-    def y_phase(s, k):
-        unit = my_unit(k)
-
-        @pl.when(unit < UNITS)
+    def y_load(s, k):
+        @pl.when(my_unit(k) < UNITS)
         def _():
             wait(U.at[s, k], a_recv.at[s, k])
             hi, lo = split2(U[s, k])
             W[:, :LANES] = hi
             W[:, LANES:] = lo
 
-            @pl.loop(0, 4)
-            def _(step):
-                m = (step + gy) % 4
+    def y_rows(s, k, begin, end):
+        unit = my_unit(k)
+
+        @pl.when(unit < UNITS)
+        def _():
+            @pl.loop(begin, end)
+            def _(t):
+                m = (y + t * (7 - t) // 2) % YR
                 rows = pl.ds(pl.multiple_of(m * 8 * ROWS, 8 * ROWS), 8 * ROWS)
                 p = jnp.dot(Yhi[rows, :], W[...], preferred_element_type=F32)
                 q = jnp.dot(Ylo[rows, :], W[:, :LANES], preferred_element_type=F32)
@@ -233,7 +235,7 @@
 
                 @pl.loop(0, 8)
                 def _(i):
-                    g = m * 8 + (i + gy // 4) % 8
+                    g = m * 8 + (i + gy) % 8
                     src = yout.at[s, k, pl.ds(pl.multiple_of(g * ROWS, ROWS), ROWS)]
                     dst = R.at[s, k, unit]
 
@@ -244,6 +246,10 @@
                     @pl.when(g == gy)
                     def _():
                         pltpu.make_async_copy(src, dst, r_recv.at[s, k]).start()
+
+    def y_phase(s, k):
+        y_load(s, k)
+        y_rows(s, k, 0, YR)
 
     def solve(s, k, lb):
         sl = slice(lb * LANES, (lb + 1) * LANES)
@@ -276,14 +282,14 @@
     def row_dev(xx):
         return (gx, xx * NZ + z)
 
-    def to_sib(ref, i):
-        rcopy(ref, ref, yb_send.at[i], yb_recv, sib).start()
+    def to_sib(ref, i, group):
+        rcopy(ref, ref, yb_send.at[i], yb_recv.at[group], sib).start()
 
     def along_x(i, yy):
         block = yblock(2 * yy + c, x)
         rcopy(block, block, yx_send.at[i, 0], yx_recv.at[i, 0], row_dev(xp)).start()
         rcopy(block, block, yx_send.at[i, 1], yx_recv.at[i, 1], row_dev(xm)).start()
-        to_sib(block, 1 + i)
+        to_sib(block, 1 + i, 1 + i)
 
     def y_near():
         for i, (yy, to) in enumerate(((ym, yp), (yp, ym))):
@@ -305,19 +311,22 @@
             wait(block, yx_recv.at[i, j])
             part = yhalf(2 * yy + c, xx, j)
             rcopy(part, part, yx_send.at[i, 2 + j], yx_recv.at[i, 2 + j], row_dev(to)).start()
-            to_sib(block, 4 + 4 * i + j)
+            to_sib(block, 4 + 4 * i + j, 1 + i)
 
     def x_far(i):
         yy = (ym, yp, yo)[i]
         for j in range(2):
             part = yhalf(2 * yy + c, xo, j)
             wait(part, yx_recv.at[i, 2 + j])
-            to_sib(part, 6 + 4 * i + j)
-
-    def y_split(cc):
-        @pl.loop(0, YR)
-        def _(j):
-            rows = pl.ds(pl.multiple_of((2 * j + cc) * YSH, YSH), YSH)
+            to_sib(part, 6 + 4 * i + j, 1 + i)
+
+    def y_split(group):
+        yy = (y, ym, yp, yo)[group]
+        wait(yblock(0, 0, NX), yb_recv.at[group])
+
+        @pl.loop(0, 2)
+        def _(cc):
+            rows = pl.ds(pl.multiple_of((2 * yy + cc) * YSH, YSH), YSH)
             hi, lo = split2(Yf[rows, :])
             Yhi[rows, :] = hi
             Ylo[rows, :] = lo
@@ -335,7 +344,7 @@
     for i, yy in enumerate((yp, ym)):
         rcopy(yrow, yblock(gx, x), ys_send.at[i], ys_recv.at[i], col(yy)).start()
     own(0, 0)
-    rcopy(yinv, yblock(gx, 0, NX), yb_send.at[0], yb_recv, sib).start()
+    rcopy(yinv, yblock(gx, 0, NX), yb_send.at[0], yb_recv.at[0], sib).start()
     for load in loads[3:]:
         load.start()
 
@@ -357,6 +366,13 @@
                 prev = kap_v[l, :, sl] * rec
                 cs[l, :, sl] = prev
 
+    def first_solve(k):
+        wait(R.at[0, k], r_recv.at[0, k])
+        for lb in range(LB):
+            u = solve(0, k, lb)
+            for l in range(LEV):
+                F[k, l, :, lb * LANES : (lb + 1) * LANES] = u[l]
+
     loads[0].wait()
     turn(0, 6)
     y_near()
@@ -365,20 +381,33 @@
     near(0, 0)
     own(0, 2)
     y_far()
-    mult(0, 0)
     near(0, 1)
     own(0, 3)
     x_near(0)
+    x_near(1)
+    far(0, 0)
+    mult(0, 0)
+    near(0, 2)
+    x_near(2)
+    far(0, 1)
     mult(0, 1)
-    near(0, 2)
-    x_near(1)
+    near(0, 3)
     x_far(0)
+    far(0, 2)
     mult(0, 2)
-    near(0, 3)
-    x_near(2)
     x_far(1)
+    far(0, 3)
+    loads[5].wait()
+    y_split(0)
+    y_split(1)
+    y_split(2)
+    y_load(0, 0)
+    y_rows(0, 0, 0, 3)
     mult(0, 3)
     x_far(2)
+    y_split(3)
+    y_rows(0, 0, 3, 4)
+    y_phase(0, 1)
 
     row = tidx[...]
     three = row >> 7
@@ -392,35 +421,27 @@
     lat = lax.broadcasted_iota(I32, (ROWS, SLOTS), 0)
     wy[...] = jnp.where(lat == trow, 1.0 - fy, jnp.where(lat == trow + 1, fy, 0.0))
 
-    loads[5].wait()
-    y_split(c)
-    wait(Yf.at[pl.ds(0, 4 * YSH)], yb_recv)
-    y_split(1 - c)
-    y_phase(0, 0)
-    y_phase(0, 1)
-
-    def first_solve(k):
-        wait(R.at[0, k], r_recv.at[0, k])
-        for lb in range(LB):
-            u = solve(0, k, lb)
-            for l in range(LEV):
-                F[k, l, :, lb * LANES : (lb + 1) * LANES] = u[l]
 
     first_solve(0)
     own(1, 0)
     own(1, 1)
     near(1, 0)
+    near(1, 1)
+    far(1, 0)
     first_solve(1)
     own(1, 2)
+    own(1, 3)
     mult(1, 0)
-    near(1, 1)
-    own(1, 3)
+    far(1, 1)
     mult(1, 1)
     near(1, 2)
+    near(1, 3)
+    far(1, 2)
     mult(1, 2)
+    far(1, 3)
+    mult(1, 3)
     y_phase(1, 0)
-    near(1, 3)
-    mult(1, 3)
+    y_phase(1, 1)
 
     loads[3].wait()
     loads[4].wait()
@@ -432,7 +453,6 @@
             inc[0, l, :, sl] = sig_v[0, l, :, sl] * u[l]
     ob_i[...] = jnp.zeros_like(ob_i)
     interp_rows(inc[0], 0)
-    y_phase(1, 1)
     wait(R.at[1, 1], r_recv.at[1, 1])
     for lb in range(LB):
         sl = slice(lb * LANES, (lb + 1) * LANES)
@@ -457,40 +477,38 @@
     rank = jnp.sum(earlier, axis=0, keepdims=True)
     live = lax.broadcasted_iota(I32, (1, SLOTS), 1) < count[0]
     values = jnp.where(live, ob_i[...], 0.0)
-    placed = jnp.concatenate(
-        [
-            jnp.where(rank == 0.0, values, 0.0),
-            jnp.where(rank == 1.0, values, 0.0),
-            jnp.zeros((LANES - 32, SLOTS), F32),
-        ],
-        axis=0,
-    )
-    target = (own_row % GY) * GX + own_row // GY
-    pick = jnp.where(ia == target, 1.0, 0.0).astype(BF16)
+    ogx, ogy = own_row // GY, own_row % GY
+    both = jnp.concatenate([jnp.where(rank == 0.0, values, 0.0), jnp.where(rank == 1.0, values, 0.0)], axis=0)
+    placed = jnp.concatenate([jnp.where(ogx % 4 == q, both, 0.0) for q in range(4)], axis=0)
     hi, mid = split2(placed)
     low = ((placed - hi.astype(F32)) - mid.astype(F32)).astype(BF16)
     dims = (((1,), (1,)), ((), ()))
-    ob_o[...] = (
-        lax.dot_general(pick, hi, dims, preferred_element_type=F32)
-        + lax.dot_general(pick, mid, dims, preferred_element_type=F32)
-    ) + lax.dot_general(pick, low, dims, preferred_element_type=F32)
+    line = lax.broadcasted_iota(I32, (GY, SLOTS), 0)
+    for h in range(2):
+        pick = jnp.where((line == ogy) & (ogx // 4 == h), 1.0, 0.0).astype(BF16)
+        ob_o[:, h, :] = (
+            lax.dot_general(pick, hi, dims, preferred_element_type=F32)
+            + lax.dot_general(pick, mid, dims, preferred_element_type=F32)
+        ) + lax.dot_general(pick, low, dims, preferred_element_type=F32)
 
     @pl.loop(0, GY)
-    def _(g):
-        src = ob_o.at[pl.ds(pl.multiple_of(g * GX, GX), GX)]
-        dst = ob_a.at[pl.ds(pl.multiple_of(gy * GX, GX), GX)]
-
-        @pl.when(g != gy)
+    def _(i):
+        g = (gy + i) % GY
+        src = ob_o.at[g]
+        dst = ob_a.at[gy]
+
+        @pl.when(i != 0)
         def _():
             rcopy(src, dst, o_send.at[0], o_recv.at[0], (gx, g)).start()
 
-        @pl.when(g == gy)
+        @pl.when(i == 0)
         def _():
             pltpu.make_async_copy(src, dst, o_recv.at[0]).start()
 
     wait(ob_a, o_recv.at[0])
     for g in range(GX):
-        ob_m[g] = ob_a[pl.ds(g, GY, stride=GX), :]
+        part = ob_a[:, g // 4, :]
+        ob_m[g] = pltpu.roll(part, (LANES - 32 * (g % 4)) % LANES, 1) if g % 4 else part
     for g in range(GX):
         src = ob_m.at[g]
         dst = ob_f.at[pl.ds(pl.multiple_of(gx * GY, GY), GY)]
@@ -505,8 +523,8 @@
 
     wait(ob_f, o_recv.at[1])
     turned = ob_f[...].T
-    obs[0] = turned[0:REC]
-    obs[1] = turned[16 : 16 + REC]
+    obs[:, 0, :] = turned[0:REC]
+    obs[:, 1, :] = turned[16 : 16 + REC]
 
     for s in range(STEPS):
         for p in range(PIECES):
@@ -533,8 +551,14 @@
             wait(yblock(0, 0) if j < 2 else yhalf(0, 0, 0), yb_send.at[4 + 4 * i + j])
         wait(yblock(0, 0), yb_send.at[1 + i])
     wait(yblock(0, 0, NX), yb_send.at[0])
-    wait(ob_o.at[pl.ds(0, (GY - 1) * GX)], o_send.at[0])
+    wait(ob_o.at[pl.ds(0, GY - 1)], o_send.at[0])
     wait(ob_m.at[pl.ds(0, GX - 1)], o_send.at[1])
+
+
+def copy_out(a, b, d, oa, ob, od):
+    oa[...] = a[...]
+    ob[...] = b[...]
+    od[...] = d[...]
 
 
 def body(
@@ -550,7 +574,7 @@
         out_shape=(
             jax.ShapeDtypeStruct((KINDS, LEV) + tile, F32),
             jax.ShapeDtypeStruct(tile, F32),
-            jax.ShapeDtypeStruct((CAP, REC, DEV), F32),
+            jax.ShapeDtypeStruct((REC, CAP, DEV), F32),
         ),
         in_specs=[hbm] * 7 + [smem, vmem, vmem, vmem, smem],
         out_specs=(vmem, vmem, vmem),
@@ -577,8 +601,8 @@
             pltpu.VMEM((COLS, 2 * SLOTS), BF16),
             pltpu.VMEM((ROWS, SLOTS), F32),
             pltpu.VMEM((16, SLOTS), F32),
-            pltpu.VMEM((DEV, LANES), F32),
-            pltpu.VMEM((DEV, LANES), F32),
+            pltpu.VMEM((GY, 2, LANES), F32),
+            pltpu.VMEM((GY, 2, LANES), F32),
             pltpu.VMEM((GX, GY, LANES), F32),
             pltpu.VMEM((DEV, LANES), F32),
             dma((STEPS, PIECES)),
@@ -590,7 +614,7 @@
             dma((3, 4)),
             dma((3, 4)),
             dma((16,)),
-            dma(()),
+            dma((4,)),
             dma((STEPS, KINDS)),
             dma((STEPS, KINDS)),
             dma((STEPS, KINDS)),
@@ -616,7 +640,15 @@
         obs_frac,
         obs_count,
     )
-    return inc[None], height[None], obs
+    results = (inc, height, obs)
+    inc, height, obs = pl.pallas_call(
+        copy_out,
+        out_shape=tuple(jax.ShapeDtypeStruct(r.shape, F32) for r in results),
+        in_specs=[vmem] * 3,
+        out_specs=(vmem,) * 3,
+        name="outputs",
+    )(*results)
+    return inc[None], height[None], jnp.swapaxes(obs, 0, 1)
 
 
 def solution(mesh):

time: 177 us -> 167 us (0.944)
  local copies, waits for them, and re-layouts: 5.04 us -> 0 us
  Pallas kernels: 170 us -> 166 us
    pallas_call x1, Pallas kernels: 170 us -> 164 us  [body(): pl.pallas_call(kernel, out_shape=(jax.ShapeDtypeStruct((KINDS, LEV) + til...]
    unnamed x3 -> x0, local copies, waits for them, and re-layouts: 5.04 us -> none
    pallas_call x0 -> x1, Pallas kernels: none -> 2.19 us  [body(): pl.pallas_call(copy_out, out_shape=tuple((jax.ShapeDtypeStruct(r.shape, F...]
where the time goes in v3:
time: 167 us
  Pallas kernels  166 us (99%)
    pallas_call x1, Pallas kernels, body(): pl.pallas_call(kernel, out_shape=(jax.ShapeDtypeStruct((KINDS, LEV) + til...  164 us

profile of v3, /device:TPU:1, one launch (start us, length us, event | category | flops | bytes accessed | tf_op | source)
XLA Modules:
  0.0 167.0 jit_solution(5724966589725728164)
XLA Ops:
  1.3 163.5 %covariance.1 = (f32[2,6,48,384]{3,2,1,0:T(8,128)}, f32[48,384]{1,0:T(8,128)}, f32[13,2,256]{2,1,0:T(2,128)}) custom-call(f32[2,6,48,384]{3,2,1,0:T(8,128)} %bitcast.6, f32[2,6,48,384]{3,2,1,0:T(8,128)} %sigma.1, f32[5,48,384]{2,1,0:T(8,128)} %kappa.1, f32[6,48,384]{2,1,0:T(8,128)} %beta.1, s32[48,384]{1,0:T(8,128)} %sea.1, f32[384,3072]{1,0:T(8,128)} %xinv.1, ...), custom_call_target="tpu_custom_call" | custom-call | tf_op jit(solution)/shard_map/covariance/pallas_call | solution.py:572
  164.8 2.2 %outputs.1 = (f32[2,6,48,384]{3,2,1,0:T(8,128)}, f32[48,384]{1,0:T(8,128)}, f32[13,2,256]{2,1,0:T(2,128)}) custom-call(f32[2,6,48,384]{3,2,1,0:T(8,128)} %get-tuple-element.9.a, f32[48,384]{1,0:T(8,128)} %get-tuple-element.10.b, f32[13,2,256]{2,1,0:T(2,128)} %get-tuple-element.11.d), custom_call_target="tpu_custom_call" | custom-call | tf_op jit(solution)/shard_map/outputs/pallas_call | solution.py:644

commit v4 on v3

--- a/solution.py
+++ b/solution.py
@@ -68,6 +68,8 @@
     sea_v,
     wx,
     wy,
+    slot,
+    picks,
     ob_i,
     ob_o,
     ob_a,
@@ -166,35 +168,35 @@
             wait(part, xs_recv.at[s, p, 3 + i])
             rcopy(part, part, xs_send.at[s, p, 7 + i], xs_recv.at[s, p, 7 + i], sib).start()
 
-    def mult(s, p):
+    def chunk(s, p, yy):
+        lhs = jnp.concatenate([G[s, p, yy, i].reshape(PLEV * ROWS, COLS) for i in range(2)], axis=1)
+        hi, lo = split2(lhs)
+        rhs = XT[pl.ds(pl.multiple_of(yy * 2 * COLS, 2 * COLS), 2 * COLS), :]
+        pr = jnp.dot(hi, rhs, preferred_element_type=F32)
+        qr = jnp.dot(lo, rhs[:, :COLS], preferred_element_type=F32)
+        return (pr[:, :COLS] + pr[:, COLS:]) + qr
+
+    def mult_near(s, p):
         wait(gat(s, p, y, c), own_sem.at[s, p])
         wait(gat(s, p, y, 1 - c), xs_recv.at[s, p, 2])
         wait(gat(s, p, ym, 1 - c), xs_recv.at[s, p, 5])
         wait(gat(s, p, yp, 1 - c), xs_recv.at[s, p, 6])
-        acc[...] = jnp.zeros_like(acc)
-
-        @pl.loop(0, YR)
+        acc[p] = jnp.zeros((PLEV * ROWS, COLS), F32)
+
+        @pl.loop(0, YR - 1)
         def _(t):
-            yy = (y + t * (t + 1) // 2) % YR
-
-            @pl.when(t == YR - 1)
-            def _():
-                for i in range(2):
-                    wait(half(gat(s, p, yo, 1 - c), i), xs_recv.at[s, p, 7 + i])
-
-            lhs = jnp.concatenate([G[s, p, yy, i].reshape(PLEV * ROWS, COLS) for i in range(2)], axis=1)
-            hi, lo = split2(lhs)
-            rhs = XT[pl.ds(pl.multiple_of(yy * 2 * COLS, 2 * COLS), 2 * COLS), :]
-            pr = jnp.dot(hi, rhs, preferred_element_type=F32)
-            qr = jnp.dot(lo, rhs[:, :COLS], preferred_element_type=F32)
-            acc[...] += (pr[:, :COLS] + pr[:, COLS:]) + qr
-
+            acc[p] += chunk(s, p, (y + t * (t + 1) // 2) % YR)
+
+    def mult_far(s, p):
+        for i in range(2):
+            wait(half(gat(s, p, yo, 1 - c), i), xs_recv.at[s, p, 7 + i])
+        total = acc[p] + chunk(s, p, yo)
         k, first = p // 2, (p % 2) * PUNITS
         for lb in range(LB):
             m = sea_v[:, lb * LANES : (lb + 1) * LANES].astype(F32)
             for f in range(PLEV):
                 xout[s, k, first + f * LB + lb] = (
-                    m * acc[f * ROWS : (f + 1) * ROWS, lb * LANES : (lb + 1) * LANES]
+                    m * total[f * ROWS : (f + 1) * ROWS, lb * LANES : (lb + 1) * LANES]
                 )
 
         @pl.loop(0, PUNITS)
@@ -381,33 +383,35 @@
     near(0, 0)
     own(0, 2)
     y_far()
+    mult_near(0, 0)
     near(0, 1)
     own(0, 3)
     x_near(0)
     x_near(1)
     far(0, 0)
-    mult(0, 0)
+    mult_far(0, 0)
+    mult_near(0, 1)
     near(0, 2)
     x_near(2)
     far(0, 1)
-    mult(0, 1)
+    mult_far(0, 1)
+    mult_near(0, 2)
     near(0, 3)
     x_far(0)
     far(0, 2)
-    mult(0, 2)
+    mult_far(0, 2)
     x_far(1)
     far(0, 3)
+    x_far(2)
     loads[5].wait()
     y_split(0)
+    mult_near(0, 3)
     y_split(1)
     y_split(2)
     y_load(0, 0)
-    y_rows(0, 0, 0, 3)
-    mult(0, 3)
-    x_far(2)
     y_split(3)
-    y_rows(0, 0, 3, 4)
-    y_phase(0, 1)
+    y_rows(0, 0, 0, 4)
+    mult_far(0, 3)
 
     row = tidx[...]
     three = row >> 7
@@ -420,26 +424,45 @@
     wx[:, SLOTS:] = wlo
     lat = lax.broadcasted_iota(I32, (ROWS, SLOTS), 0)
     wy[...] = jnp.where(lat == trow, 1.0 - fy, jnp.where(lat == trow + 1, fy, 0.0))
+    own_row = owner[...]
+    ia = lax.broadcasted_iota(I32, (SLOTS, SLOTS), 0)
+    ib = lax.broadcasted_iota(I32, (SLOTS, SLOTS), 1)
+    own_f = own_row.astype(F32)
+    own_col = jnp.sum(jnp.where(ia == ib, own_f, 0.0), axis=1, keepdims=True)
+    earlier = jnp.where((own_col == own_f) & (ia < ib), 1.0, 0.0)
+    rank = jnp.sum(earlier, axis=0, keepdims=True)
+    live = lax.broadcasted_iota(I32, (1, SLOTS), 1) < count[0]
+    ogx, ogy = own_row // GY, own_row % GY
+    slot[0:1, :] = jnp.where(live, rank, -1.0)
+    slot[1:2, :] = (ogx % 4).astype(F32)
+    line = lax.broadcasted_iota(I32, (GY, SLOTS), 0)
+    for h in range(2):
+        picks[h] = jnp.where((line == ogy) & (ogx // 4 == h), 1.0, 0.0).astype(BF16)
 
 
     first_solve(0)
     own(1, 0)
     own(1, 1)
+    y_phase(0, 1)
     near(1, 0)
+    mult_near(1, 0)
     near(1, 1)
-    far(1, 0)
     first_solve(1)
     own(1, 2)
     own(1, 3)
-    mult(1, 0)
+    far(1, 0)
+    mult_far(1, 0)
+    mult_near(1, 1)
     far(1, 1)
-    mult(1, 1)
+    mult_far(1, 1)
     near(1, 2)
+    mult_near(1, 2)
     near(1, 3)
     far(1, 2)
-    mult(1, 2)
+    mult_far(1, 2)
     far(1, 3)
-    mult(1, 3)
+    mult_near(1, 3)
+    mult_far(1, 3)
     y_phase(1, 0)
     y_phase(1, 1)
 
@@ -468,43 +491,26 @@
     interp_rows(inc[1], LEV)
     interp_rows(height[...], 2 * LEV)
 
-    own_row = owner[...]
-    ia = lax.broadcasted_iota(I32, (SLOTS, SLOTS), 0)
-    ib = lax.broadcasted_iota(I32, (SLOTS, SLOTS), 1)
-    own_f = own_row.astype(F32)
-    own_col = jnp.sum(jnp.where(ia == ib, own_f, 0.0), axis=1, keepdims=True)
-    earlier = jnp.where((own_col == own_f) & (ia < ib), 1.0, 0.0)
-    rank = jnp.sum(earlier, axis=0, keepdims=True)
-    live = lax.broadcasted_iota(I32, (1, SLOTS), 1) < count[0]
-    values = jnp.where(live, ob_i[...], 0.0)
-    ogx, ogy = own_row // GY, own_row % GY
+    rank, quarter = slot[0:1, :], slot[1:2, :]
+    values = ob_i[...]
     both = jnp.concatenate([jnp.where(rank == 0.0, values, 0.0), jnp.where(rank == 1.0, values, 0.0)], axis=0)
-    placed = jnp.concatenate([jnp.where(ogx % 4 == q, both, 0.0) for q in range(4)], axis=0)
+    placed = jnp.concatenate([jnp.where(quarter == q, both, 0.0) for q in range(4)], axis=0)
     hi, mid = split2(placed)
     low = ((placed - hi.astype(F32)) - mid.astype(F32)).astype(BF16)
     dims = (((1,), (1,)), ((), ()))
-    line = lax.broadcasted_iota(I32, (GY, SLOTS), 0)
     for h in range(2):
-        pick = jnp.where((line == ogy) & (ogx // 4 == h), 1.0, 0.0).astype(BF16)
+        pick = picks[h]
         ob_o[:, h, :] = (
             lax.dot_general(pick, hi, dims, preferred_element_type=F32)
             + lax.dot_general(pick, mid, dims, preferred_element_type=F32)
         ) + lax.dot_general(pick, low, dims, preferred_element_type=F32)
 
-    @pl.loop(0, GY)
+    @pl.loop(1, GY)
     def _(i):
         g = (gy + i) % GY
-        src = ob_o.at[g]
-        dst = ob_a.at[gy]
-
-        @pl.when(i != 0)
-        def _():
-            rcopy(src, dst, o_send.at[0], o_recv.at[0], (gx, g)).start()
-
-        @pl.when(i == 0)
-        def _():
-            pltpu.make_async_copy(src, dst, o_recv.at[0]).start()
-
+        rcopy(ob_o.at[g], ob_a.at[gy], o_send.at[0], o_recv.at[0], (gx, g)).start()
+
+    pltpu.make_async_copy(ob_o.at[gy], ob_a.at[gy], o_recv.at[0]).start()
     wait(ob_a, o_recv.at[0])
     for g in range(GX):
         part = ob_a[:, g // 4, :]
@@ -590,7 +596,7 @@
             pltpu.VMEM((STEPS, KINDS, UNITS, ROWS, LANES), F32),
             pltpu.VMEM((STEPS, KINDS, NLAT, LANES), F32),
             pltpu.VMEM((KINDS, LEV) + tile, F32),
-            pltpu.VMEM((PLEV * ROWS, COLS), F32),
+            pltpu.VMEM((PIECES, PLEV * ROWS, COLS), F32),
             pltpu.VMEM((NLAT, 2 * LANES), BF16),
             pltpu.VMEM((LEV - 1,) + tile, F32),
             pltpu.VMEM((LEV,) + tile, F32),
@@ -600,6 +606,8 @@
             pltpu.VMEM(tile, I32),
             pltpu.VMEM((COLS, 2 * SLOTS), BF16),
             pltpu.VMEM((ROWS, SLOTS), F32),
+            pltpu.VMEM((8, SLOTS), F32),
+            pltpu.VMEM((2, GY, SLOTS), BF16),
             pltpu.VMEM((16, SLOTS), F32),
             pltpu.VMEM((GY, 2, LANES), F32),
             pltpu.VMEM((GY, 2, LANES), F32),

time: 167 us -> 163 us (0.976)
  Pallas kernels: 166 us -> 162 us
    pallas_call x1, Pallas kernels: 164 us -> 160 us  [body(): pl.pallas_call(kernel, out_shape=(jax.ShapeDtypeStruct((KINDS, LEV) + til...]
where the time goes in v4:
time: 163 us
  Pallas kernels  162 us (99%)
    pallas_call x1, Pallas kernels, body(): pl.pallas_call(kernel, out_shape=(jax.ShapeDtypeStruct((KINDS, LEV) + til...  160 us

profile of v4, /device:TPU:1, one launch (start us, length us, event | category | flops | bytes accessed | tf_op | source)
XLA Modules:
  0.0 163.0 jit_solution(6662675494970887441)
XLA Ops:
  1.3 159.6 %covariance.1 = (f32[2,6,48,384]{3,2,1,0:T(8,128)}, f32[48,384]{1,0:T(8,128)}, f32[13,2,256]{2,1,0:T(2,128)}) custom-call(f32[2,6,48,384]{3,2,1,0:T(8,128)} %bitcast.6, f32[2,6,48,384]{3,2,1,0:T(8,128)} %sigma.1, f32[5,48,384]{2,1,0:T(8,128)} %kappa.1, f32[6,48,384]{2,1,0:T(8,128)} %beta.1, s32[48,384]{1,0:T(8,128)} %sea.1, f32[384,3072]{1,0:T(8,128)} %xinv.1, ...), custom_call_target="tpu_custom_call" | custom-call | tf_op jit(solution)/shard_map/covariance/pallas_call | solution.py:578
  160.8 2.2 %outputs.1 = (f32[2,6,48,384]{3,2,1,0:T(8,128)}, f32[48,384]{1,0:T(8,128)}, f32[13,2,256]{2,1,0:T(2,128)}) custom-call(f32[2,6,48,384]{3,2,1,0:T(8,128)} %get-tuple-element.9.a, f32[48,384]{1,0:T(8,128)} %get-tuple-element.10.b, f32[13,2,256]{2,1,0:T(2,128)} %get-tuple-element.11.d), custom_call_target="tpu_custom_call" | custom-call | tf_op jit(solution)/shard_map/outputs/pallas_call | solution.py:652

commit v5 on v4

--- a/solution.py
+++ b/solution.py
@@ -44,9 +44,11 @@
     tidx,
     frac,
     count,
+    inc_o,
+    height_o,
+    obs,
     inc,
     height,
-    obs,
     G,
     XT,
     xbuf,
@@ -91,6 +93,7 @@
     r_recv,
     o_send,
     o_recv,
+    out_sem,
 ):
     gx, gy = lax.axis_index("gx"), lax.axis_index("gy")
     y, c = gx // 2, gx % 2
@@ -488,6 +491,12 @@
             term = ssh[0, l] * t + ssh[1, l] * v
             h = term if h is None else h + term
         height[:, sl] = h
+    writes = [
+        pltpu.make_async_copy(inc, inc_o, out_sem.at[0]),
+        pltpu.make_async_copy(height, height_o, out_sem.at[1]),
+    ]
+    for write in writes:
+        write.start()
     interp_rows(inc[1], LEV)
     interp_rows(height[...], 2 * LEV)
 
@@ -515,7 +524,6 @@
     for g in range(GX):
         part = ob_a[:, g // 4, :]
         ob_m[g] = pltpu.roll(part, (LANES - 32 * (g % 4)) % LANES, 1) if g % 4 else part
-    for g in range(GX):
         src = ob_m.at[g]
         dst = ob_f.at[pl.ds(pl.multiple_of(gx * GY, GY), GY)]
 
@@ -532,6 +540,8 @@
     obs[:, 0, :] = turned[0:REC]
     obs[:, 1, :] = turned[16 : 16 + REC]
 
+    for write in writes:
+        write.wait()
     for s in range(STEPS):
         for p in range(PIECES):
             whole = gat(s, p, y, c)
@@ -583,8 +593,10 @@
             jax.ShapeDtypeStruct((REC, CAP, DEV), F32),
         ),
         in_specs=[hbm] * 7 + [smem, vmem, vmem, vmem, smem],
-        out_specs=(vmem, vmem, vmem),
+        out_specs=(hbm, hbm, vmem),
         scratch_shapes=[
+            pltpu.VMEM((KINDS, LEV) + tile, F32),
+            pltpu.VMEM(tile, F32),
             pltpu.VMEM((STEPS, PIECES, YR, 2, PLEV) + tile, F32),
             pltpu.VMEM((NLON, 2 * COLS), BF16),
             pltpu.VMEM((COLS, NLON), F32),
@@ -629,6 +641,7 @@
             dma((STEPS, KINDS)),
             dma((2,)),
             dma((2,)),
+            dma((2,)),
         ],
         compiler_params=pltpu.CompilerParams(
             collective_id=0, has_side_effects=True, vmem_limit_bytes=62 * 1024 * 1024

time: 163 us -> 164 us (level)
  no operation moved by 1% of the time
where the time goes in v5:
time: 164 us
  Pallas kernels  162 us (99%)
    pallas_call x1, Pallas kernels, body(): pl.pallas_call(kernel, out_shape=(jax.ShapeDtypeStruct((KINDS, LEV) + til...  160 us

profile of v5, /device:TPU:1, one launch (start us, length us, event | category | flops | bytes accessed | tf_op | source)
XLA Modules:
  0.0 163.5 jit_solution(4096622058561113708)
XLA Ops:
  1.3 160.0 %covariance.1 = (f32[2,6,48,384]{3,2,1,0:T(8,128)}, f32[48,384]{1,0:T(8,128)}, f32[13,2,256]{2,1,0:T(2,128)}) custom-call(f32[2,6,48,384]{3,2,1,0:T(8,128)} %bitcast.6, f32[2,6,48,384]{3,2,1,0:T(8,128)} %sigma.1, f32[5,48,384]{2,1,0:T(8,128)} %kappa.1, f32[6,48,384]{2,1,0:T(8,128)} %beta.1, s32[48,384]{1,0:T(8,128)} %sea.1, f32[384,3072]{1,0:T(8,128)} %xinv.1, ...), custom_call_target="tpu_custom_call" | custom-call | tf_op jit(solution)/shard_map/covariance/pallas_call | solution.py:588
  161.3 2.2 %outputs.1 = (f32[2,6,48,384]{3,2,1,0:T(8,128)}, f32[48,384]{1,0:T(8,128)}, f32[13,2,256]{2,1,0:T(2,128)}) custom-call(f32[2,6,48,384]{3,2,1,0:T(8,128)} %get-tuple-element.9.a, f32[48,384]{1,0:T(8,128)} %get-tuple-element.10.b, f32[13,2,256]{2,1,0:T(2,128)} %get-tuple-element.11.d), custom_call_target="tpu_custom_call" | custom-call | tf_op jit(solution)/shard_map/outputs/pallas_call | solution.py:665
